TPU v7x, 256 devices: a whole 4x4x8 slice. The times are simulated.
256 devices in a mesh: width: 8 (over y, core), hidden: 32 (over z, x).
Axes of the slice: x: 4, y: 4, z: 8, core: 2. Of those that a mesh axis runs over, the one named last changes fastest.
Arguments:
- tokens: bfloat16 [1152, 5120], P(None, 'width'), may hold values from -6 to 6
- cotangent: bfloat16 [1152, 5120], P(None, 'width'), may hold values from -6 to 6
- w_up: bfloat16 [5120, 13824], P('width', 'hidden'), may hold values from -0.078125 to 0.078125
- bias_up: float32 [13824], P('hidden'), may hold values from -3 to 3
- w_down: bfloat16 [13824, 5120], P('hidden', 'width'), may hold values from -0.0546875 to 0.0546875
- mod_table: float32 [32, 3, 5120], P(None, None, 'width'), may hold values from -3 to 3
- seg_ids: int32 [1152], replicated, may hold values from 0 to 15, never falling along the last dimension, each value on 1 to 144 neighbouring positions
- step_ids: int32 [16], replicated, may hold values from 0 to 31
Outputs:
- grad_x: bfloat16 [1152, 5120], P(None, 'width')
- grad_up: float32 [5120, 13824], P('width', 'hidden')
- grad_down: float32 [13824, 5120], P('hidden', 'width')
- grad_bias: float32 [13824], P('hidden')
- grad_table: float32 [32, 3, 5120], P(None, None, 'width')
Inputs may be any that keep to these rules, and one draw needn't show every extreme that they name: `seg_ids`: request numbers never fall along the tokens and every request holds at least one token.
All inputs are finite; a program needn't handle non-finite values.
Results may differ from a plain program's by a relative error of at most 0.0063.
Values may be sent and summed in bfloat16 or wider, within the bound.
A program may use at most 64 MiB of HBM per device.

v0:
```python
import jax
import jax.numpy as jnp
from jax import lax
from jax.sharding import PartitionSpec as P

D = 5120


def gelu_tanh(value):
    return jax.nn.gelu(value, approximate=True)


def norm_back(d_norm, x_hat, mod_gain, inv_std, cotangent):
    d_hat = d_norm * mod_gain
    feature_sums = lax.psum((jnp.sum(d_hat, 1), jnp.sum(d_hat * x_hat, 1)), "width")
    mean_one = feature_sums[0] / D
    mean_two = feature_sums[1] / D
    grad_rows = cotangent.astype(jnp.float32) + inv_std[:, None] * (
        d_hat - mean_one[:, None] - x_hat * mean_two[:, None]
    )
    return grad_rows.astype(jnp.bfloat16)


def per_device(tokens, cotangent, w_up, bias_up, w_down, mod_table, seg_ids, step_ids):
    highest = lax.Precision.HIGHEST
    req_count = step_ids.shape[0]
    table_rows = mod_table.shape[0]
    req_of = (seg_ids[:, None] == jnp.arange(req_count)[None, :]).astype(jnp.float32)
    step_of = (step_ids[:, None] == jnp.arange(table_rows)[None, :]).astype(jnp.float32)
    req_mod = jnp.einsum("rk,kcd->rcd", step_of, mod_table, precision=highest)
    shift_tok = jnp.dot(req_of, req_mod[:, 0], precision=highest)
    scale_tok = jnp.dot(req_of, req_mod[:, 1], precision=highest)
    gate_tok = jnp.dot(req_of, req_mod[:, 2], precision=highest)
    x_full = tokens.astype(jnp.float32)
    moment_one, moment_two = lax.psum((jnp.sum(x_full, 1), jnp.sum(x_full * x_full, 1)), "width")
    tok_mean = moment_one / D
    tok_var = moment_two / D - tok_mean * tok_mean
    inv_std = lax.rsqrt(tok_var + 1e-06)
    x_hat = (x_full - tok_mean[:, None]) * inv_std[:, None]
    mod_gain = 1.0 + scale_tok
    normed = (x_hat * mod_gain + shift_tok).astype(jnp.bfloat16)
    up_part = jnp.dot(normed, w_up, preferred_element_type=jnp.float32)
    pre_share = lax.psum(up_part, "width") + bias_up
    hidden_act = gelu_tanh(pre_share).astype(jnp.bfloat16)
    y_part = jnp.dot(hidden_act, w_down, preferred_element_type=jnp.float32)
    gate_part = jnp.dot(req_of.T, cotangent.astype(jnp.float32) * y_part, precision=highest)
    d_out = (cotangent.astype(jnp.float32) * gate_tok).astype(jnp.bfloat16)
    down_part = jnp.dot(d_out, w_down.T, preferred_element_type=jnp.float32)
    act_grad = lax.psum(down_part, "width")
    _, pull = jax.vjp(gelu_tanh, pre_share)
    pre_grad = pull(act_grad)[0]
    grad_bias = jnp.sum(pre_grad, 0)
    d_pre_b = pre_grad.astype(jnp.bfloat16)
    grad_down = jnp.dot(hidden_act.T, d_out, preferred_element_type=jnp.float32)
    grad_up = jnp.dot(normed.T, d_pre_b, preferred_element_type=jnp.float32)
    d_part = jnp.dot(d_pre_b, w_up.T, preferred_element_type=jnp.float32)
    shift_part = jnp.dot(req_of.T, d_part, precision=highest)
    scale_part = jnp.dot(req_of.T, d_part * x_hat, precision=highest)
    req_grads = lax.psum(jnp.stack([shift_part, scale_part, gate_part], 1), "hidden")
    grad_table = jnp.einsum("rk,rcd->kcd", step_of, req_grads, precision=highest)
    d_norm = lax.psum(d_part, "hidden")
    grad_x = norm_back(d_norm, x_hat, mod_gain, inv_std, cotangent)
    return (grad_x, grad_up, grad_down, grad_bias, grad_table)


def solution(mesh):
    placed = (
        P(None, "width"),
        P(None, "width"),
        P("width", "hidden"),
        P("hidden"),
        P("hidden", "width"),
        P(None, None, "width"),
        P(),
        P(),
    )
    return jax.shard_map(
        per_device,
        mesh=mesh,
        in_specs=placed,
        out_specs=(
            P(None, "width"),
            P("width", "hidden"),
            P("hidden", "width"),
            P("hidden"),
            P(None, None, "width"),
        ),
        check_vma=False,
    )
```

profile of v0, /device:TPU:8, one launch (start us, length us, event | category | flops | bytes accessed | tf_op | source)
XLA Modules:
  0.0 337.0 jit_solution(2500453837761555795)
XLA Ops:
  7.2 0.0 copy-start
  7.2 0.0 all-reduce.9.cloned.1.call-start
  7.2 1.9 fusion.3
  9.2 0.0 copy-start.9
  9.2 0.0 copy-start.18
  9.2 1.3 fusion.38
  10.5 0.0 copy-start.17
  10.5 2.1 convolution_add_fusion.1
  12.7 0.0 copy-done.9
  12.7 0.0 copy-done.18
  12.7 0.0 copy-start.5
  12.7 2.6 fusion
  15.3 0.0 copy-done.17
  15.3 22.8 %all-reduce.2 = (f32[1152]{0:T(1024)S(1)}, f32[1152]{0:T(1024)S(1)}) all-reduce(f32[1152]{0:T(1024)S(1)} %get-tuple-element.8, f32[1152]{0:T(1024)S(1)} %get-tuple-element.7), channel_id=1, replica_groups=mesh['width'=8,'hidden'=32] {'width'}, use_global_device_ids=true, to_apply=%region_3.0 | all-reduce | flops 2304 | bytes 18432 | tf_op jit(solution)/shard_map/psum | solution.py:35
  38.1 0.0 copy-done
  38.1 0.0 copy-start.2
  38.2 3.9 %fusion.46 = f32[1152,432]{0,1:T(8,128)} fusion(bf16[1152,640]{1,0:T(8,128)(2,1)} %fusion, bf16[432,640]{1,0:T(8,128)(2,1)S(1)} %copy-done), kind=kOutput, calls=%fused_computation.63 | convolution fusion | flops 637009920 | bytes 4018176 | tf_op jit(solution)/shard_map/dot_general | solution.py:48
  42.0 0.0 copy-done.5
  42.0 0.0 copy-done.2
  42.0 3.3 fusion.1
  45.3 0.0 copy-start.7
  45.3 1.1 copy-done.7
  46.4 0.0 copy-done.12
  46.4 2.3 fusion.47
  48.8 0.0 all-reduce.9.cloned.1.call-update
  48.8 0.2 all-reduce.7.cloned.1.call-start
  49.0 77.6 %all-reduce.9.cloned.1.call-done = (f32[1152,432]{0,1:T(8,128)}, f32[1152,432]{0,1:T(8,128)}) async-done(((f32[1152,432]{0,1:T(8,128)}, f32[1152,432]{0,1:T(8,128)}), (f32[1152,432]{0,1:T(8,128)}, f32[1152,432]{0,1:T(8,128)})) %all-reduce.9.cloned.1.call-update) | async-done | bytes 3981328 | tf_op jit(solution)/shard_map/psum | solution.py:49
  126.6 0.0 copy-done.20
  126.6 3.2 convert_multiply_fusion.1
  129.9 0.0 copy-start.13
  129.9 2.2 fusion.44
  132.1 1.1 fusion.27
  133.3 0.2 copy-done.3
  133.5 1.6 fusion.22
  135.1 1.3 convolution_bitcast_fusion.1
  136.4 1.3 convolution_bitcast_fusion
  137.7 0.7 pad_maximum_fusion
  138.3 0.0 all-reduce.7.cloned.1.call-update
  138.4 0.7 copy-done.8
  139.1 2.0 fusion.25
  141.1 0.0 copy-done.15
  141.1 2.5 fusion.42
  143.6 156.1 %all-reduce.7.cloned.1.call-done = (f32[1152,640]{1,0:T(8,128)}, f32[16,3,640]{2,0,1:T(8,128)}) async-done(((f32[1152,640]{1,0:T(8,128)}, f32[16,3,640]{2,0,1:T(8,128)}), (f32[1152,640]{1,0:T(8,128)}, f32[16,3,640]{2,0,1:T(8,128)})) %all-reduce.7.cloned.1.call-update) | async-done | bytes 3072016 | tf_op jit(solution)/shard_map/psum | solution.py:61
  299.7 5.3 %fusion.43 = (f32[1152]{0:T(1024)S(1)}, f32[1152]{0:T(1024)S(1)}, f32[1152,640]{1,0:T(8,128)}) fusion(f32[1152]{0:T(1024)S(1)} %get-tuple-element.21, f32[1152]{0:T(1024)S(1)} %get-tuple-element.20, bf16[1152,640]{1,0:T(8,128)(2,1)S(1)} %copy-done.4, f32[1152,640]{1,0:T(8,128)} %get-tuple-element.9, f32[1152,640]{1,0:T(8,128)} %copy-done.5), kind=kLoop, calls=%fused_computation.61 | loop fusion | flops 5158656 | bytes 10340352 | tf_op jit(solution)/shard_map/reduce_sum | solution.py:15
  305.0 0.0 copy-done.21
  305.0 1.1 fusion.36
  306.1 20.6 %all-reduce.1 = (f32[1152]{0:T(1024)S(1)}, f32[1152]{0:T(1024)S(1)}) all-reduce(f32[1152]{0:T(1024)S(1)} %get-tuple-element.6, f32[1152]{0:T(1024)S(1)} %get-tuple-element.5), channel_id=1, replica_groups=mesh['width'=8,'hidden'=32] {'width'}, use_global_device_ids=true, to_apply=%region_10.0 | all-reduce | flops 2304 | bytes 18432 | tf_op jit(solution)/shard_map/psum | solution.py:15
  326.7 3.5 %fusion.2 = bf16[1152,640]{1,0:T(8,128)(2,1)} fusion(bf16[1152,640]{1,0:T(8,128)(2,1)S(1)} %copy-done.11, bf16[1152,640]{1,0:T(8,128)(2,1)S(1)} %copy-done.4, f32[1152,640]{1,0:T(8,128)} %get-tuple-element.19, f32[1152]{0:T(1024)S(1)} %get-tuple-element.22, f32[1152]{0:T(1024)S(1)} %get-tuple-element.23, f32[1152]{0:T(1024)S(1)} %get-tuple-element.20, ...), kind=kLoop, calls=%fused_computation.10 | loop fusion | flops 7372800 | bytes 7391232 | tf_op jit(solution)/shard_map/convert_element_type | solution.py:21
  (25 shorter events, 0.1 us)
Async XLA Ops:
  7.2 31.0 %copy-start = (bf16[432,640]{1,0:T(8,128)(2,1)S(1)}, bf16[432,640]{1,0:T(8,128)(2,1)}, u32[]{:S(2)}) copy-start(bf16[432,640]{1,0:T(8,128)(2,1)} %param.12) | copy-start | bytes 1658884
  7.2 119.4 %all-reduce.9.cloned.1.call-start = ((), (), s32[]{:S(2)}) async-start(), calls=%async_computation.1 | async-start | bytes 7962624 | tf_op jit(solution)/shard_map/psum | solution.py:49
  9.2 3.5 %copy-start.9 = (bf16[1152,640]{1,0:T(8,128)(2,1)S(1)}, bf16[1152,640]{1,0:T(8,128)(2,1)}, u32[]{:S(2)}) copy-start(bf16[1152,640]{1,0:T(8,128)(2,1)} %param.9) | copy-start | bytes 4423684
  9.2 3.5 %copy-start.18 = (s32[1152]{0:T(1024)S(1)}, s32[1152]{0:T(1024)}, u32[]{:S(2)}) copy-start(s32[1152]{0:T(1024)} %param.14) | copy-start | bytes 13828
  10.5 4.8 %copy-start.17 = (f32[16,3,640]{2,0,1:T(8,128)}, f32[16,3,640]{2,0,1:T(8,128)S(1)}, u32[]{:S(2)}) copy-start(f32[16,3,640]{2,0,1:T(8,128)S(1)} %fusion.38) | copy-start | bytes 368644
  12.7 29.3 %copy-start.5 = (f32[1152,640]{1,0:T(8,128)}, f32[1152,640]{1,0:T(8,128)S(1)}, u32[]{:S(2)}) copy-start(f32[1152,640]{1,0:T(8,128)S(1)} %convolution_add_fusion.1) | copy-start | bytes 8847364
  38.1 3.9 %copy-start.2 = (bf16[1152,640]{1,0:T(8,128)(2,1)S(1)}, bf16[1152,640]{1,0:T(8,128)(2,1)}, u32[]{:S(2)}) copy-start(bf16[1152,640]{1,0:T(8,128)(2,1)} %param.8) | copy-start | bytes 4423684
  42.0 4.4 %copy-start.12 = (bf16[640,432]{0,1:T(8,128)(2,1)S(1)}, bf16[640,432]{0,1:T(8,128)(2,1)}, u32[]{:S(2)}) copy-start(bf16[640,432]{0,1:T(8,128)(2,1)} %param.10) | copy-start | bytes 1658884
  45.3 1.1 copy-start.7
  48.8 77.9 %copy-start.10 = (bf16[1152,640]{1,0:T(8,128)(2,1)S(1)}, bf16[1152,640]{1,0:T(8,128)(2,1)}, u32[]{:S(2)}) copy-start(bf16[1152,640]{1,0:T(8,128)(2,1)} %param.9) | copy-start | bytes 4423684
  48.8 77.9 %copy-start.20 = (f32[432]{0:T(512)S(1)}, f32[432]{0:T(512)}, u32[]{:S(2)}) copy-start(f32[432]{0:T(512)} %param.11) | copy-start | bytes 5188
  48.8 250.9 %all-reduce.7.cloned.1.call-start = ((), (), s32[]{:S(2)}) async-start(), calls=%async_computation | async-start | bytes 6144000 | tf_op jit(solution)/shard_map/psum | solution.py:61
  126.6 3.2 copy-start.14
  126.6 3.2 copy-start.16
  129.9 2.2 copy-start.13
  132.1 1.4 copy-start.3
  133.5 1.6 copy-start.1
  137.7 1.4 copy-start.8
  139.1 2.0 copy-start.6
  139.1 2.0 copy-start.15
  141.1 158.5 %copy-start.4 = (bf16[1152,640]{1,0:T(8,128)(2,1)S(1)}, bf16[1152,640]{1,0:T(8,128)(2,1)}, u32[]{:S(2)}) copy-start(bf16[1152,640]{1,0:T(8,128)(2,1)} %param.8) | copy-start | bytes 4423684
  299.7 5.3 %copy-start.19 = (f32[16,3,640]{2,0,1:T(8,128)S(1)}, f32[16,3,640]{2,0,1:T(8,128)}, u32[]{:S(2)}) copy-start(f32[16,3,640]{2,0,1:T(8,128)} %get-tuple-element.10) | copy-start | bytes 368644
  299.7 5.3 %copy-start.21 = (s32[16]{0:T(128)S(1)}, s32[16]{0:T(128)}, u32[]{:S(2)}) copy-start(s32[16]{0:T(128)} %param.15) | copy-start | bytes 196
  299.7 27.0 %copy-start.11 = (bf16[1152,640]{1,0:T(8,128)(2,1)S(1)}, bf16[1152,640]{1,0:T(8,128)(2,1)}, u32[]{:S(2)}) copy-start(bf16[1152,640]{1,0:T(8,128)(2,1)} %param.9) | copy-start | bytes 4423684
Sparse Core Ops, SparseCore 0:
  48.9 77.6 all-reduce.8
  138.5 161.1 all-reduce.6
where the time goes:
time: 339 us; the launch traced here: 337 us
  waiting for transfers between devices  234 us (69%)
  blocking collectives  43.5 us (13%)
  matrix products  29.6 us (9%)
  between operations  14.2 us (4%)
  other arithmetic  13.7 us (4%)
    psum x1, waiting for transfers between devices, per_device(): d_norm = lax.psum(d_part, 'hidden')  156 us
    psum x1, waiting for transfers between devices, per_device(): act_grad = lax.psum(down_part, 'width')  77.6 us
    psum x1, blocking collectives, per_device(): lax.psum((jnp.sum(x_full, 1), jnp.sum(x_full * x_full, 1)), 'width')  22.8 us
    psum x1, blocking collectives, norm_back(): lax.psum((jnp.sum(d_hat, 1), jnp.sum(d_hat * x_hat, 1)), 'width')  20.6 us
  transfers between devices with their start and end apart: 2, of which 2 were waited for; matrix products, arithmetic and copies ran while one was open for 1% of the time, Pallas kernels for 0%

commit v1 on v0

v1 whole, which is shorter than its diff:
```python
import functools

import jax
import jax.numpy as jnp
from jax import lax
from jax.experimental import pallas as pl
from jax.experimental.pallas import tpu as pltpu
from jax.sharding import PartitionSpec as P

MESH = pl.DeviceIdType.MESH
F32, BF16 = jnp.float32, jnp.bfloat16

T, DW, FW, R, NS = 1152, 640, 432, 16, 32
D = 5120
CH = 144
HALF = 576
OWN = 48
CUT = 384
ROOT = 0.7978845608028654
CUBE = 0.044715


def split3(v):
    hi = v.astype(BF16)
    rest = v - hi.astype(F32)
    mid = rest.astype(BF16)
    return hi, mid, (rest - mid.astype(F32)).astype(BF16)


def dot(a, b, dims=((1,), (0,))):
    return lax.dot_general(a, b, (dims, ((), ())), preferred_element_type=F32)


def rows_at(start, size, step=16):
    return pl.ds(pl.multiple_of(start, step), size)


def kernel(
    tok, cot, wup, bias, wdn, tab, seg, stp,
    gx, gup, gdn, gb, gtab,
    stat, rmod, oh, oht, col, dout, nrm,
    psib, rsib, pown, ysum, yrec, had,
    dn, sb, rb, zsum, xs, xr, mst,
    tl, tx, ts, tz, tf,
    st_s, st_r, cx_s, cx_r, yr_s, yr_r, ya_s, ya_r, fw_s, fw_r,
    zr_s, zr_r, xe_s, xe_r, ms_s, ms_r, xg_s, xg_r, zg_s, zg_r,
    tx_s, tx_r, tz_s, tz_r, tg_s, tg_r,
):
    w = lax.axis_index("width")
    h = lax.axis_index("hidden")
    y, c = w // 2, w % 2
    z, x = h // 4, h % 4

    def at_w(d):
        return ((w + d) % 8, h)

    def at_y(d):
        return (((y + d) % 4) * 2 + c, h)

    sib = (y * 2 + 1 - c, h)

    def at_z(d):
        return (w, ((z + d) % 8) * 4 + x)

    def at_x(d):
        return (w, z * 4 + (x + d) % 4)

    def send(src, dst, s_sem, r_sem, dev):
        return pltpu.make_async_remote_copy(
            src_ref=src, dst_ref=dst, send_sem=s_sem, recv_sem=r_sem, device_id=dev, device_id_type=MESH
        )

    bar = pltpu.get_barrier_semaphore()
    for d in range(1, 8):
        pl.semaphore_signal(bar, inc=1, device_id=at_w(d), device_id_type=MESH)
        pl.semaphore_signal(bar, inc=1, device_id=at_z(d), device_id_type=MESH)
    for d in range(1, 4):
        pl.semaphore_signal(bar, inc=1, device_id=at_x(d), device_id_type=MESH)

    @pl.loop(0, 9)
    def _(b):
        v = tok[rows_at(b * 128, 128, 128), :].astype(F32)
        s1 = v[:, 0:128]
        s2 = v[:, 0:128] * v[:, 0:128]
        for k in range(1, 5):
            p = v[:, k * 128 : (k + 1) * 128]
            s1 = s1 + p
            s2 = s2 + p * p
        lanes = rows_at(b * 128, 128, 128)
        stat[w, 0:1, lanes] = jnp.sum(s1.T, 0, keepdims=True)
        stat[w, 1:2, lanes] = jnp.sum(s2.T, 0, keepdims=True)

    pl.semaphore_wait(bar, 17)

    st_cp = [send(stat.at[w], stat.at[w], st_s.at[d - 1], st_r.at[d - 1], at_w(d)) for d in range(1, 8)]
    for cp in st_cp:
        cp.start()

    step_of = (stp[...] == lax.broadcasted_iota(jnp.int32, (R, NS), 1)).astype(F32).astype(BF16)
    for k in range(3):
        parts = split3(tab[:, k, :])
        rm = dot(step_of, parts[0]) + dot(step_of, parts[1]) + dot(step_of, parts[2])
        for i, part in enumerate(split3(rm)):
            rmod[k, i * R : (i + 1) * R, :] = part
    oht[...] = (seg[...] == lax.broadcasted_iota(jnp.int32, (R, T), 0)).astype(F32).astype(BF16)

    @pl.loop(0, 9)
    def _(b):
        lanes = rows_at(b * 128, 128, 128)
        one = (seg[:, lanes] == lax.broadcasted_iota(jnp.int32, (R, 128), 0)).astype(F32)
        three = jnp.concatenate([one, one, one], 0)
        oh[lanes, :] = three.T.astype(BF16)
        gate = dot(oh[lanes, :], rmod[2])
        dout[lanes, :] = (cot[lanes, :].astype(F32) * gate).astype(BF16)

    def width_reduce(a, left, right, dims):
        @pl.loop(0, 2)
        def _(k):
            p = dot(left[rows_at((1 - c) * HALF + k * 288, 288), :], right[...], dims).astype(BF16)
            psib[a, 2 * k] = p[0:CH]
            psib[a, 2 * k + 1] = p[CH:288]

        cx = send(psib.at[a], rsib.at[a], cx_s.at[a], cx_r.at[a], sib)
        cx.start()

        @pl.loop(0, 2)
        def _(k):
            p = dot(left[rows_at(c * HALF + k * 288, 288), :], right[...], dims)
            pown[2 * k] = p[0:CH]
            pown[2 * k + 1] = p[CH:288]

        cx.wait()

        @pl.loop(0, 4)
        def _(k):
            ysum[a, k] = (pown[k] + rsib[a, k].astype(F32)).astype(BF16)

        cps = []
        for d in (2, 1, 3):
            cp = send(ysum.at[a, (y + d) % 4], yrec.at[a, d - 1], yr_s.at[a, d - 1], yr_r.at[a, d - 1], at_y(d))
            cp.start()
            cps.append(cp)
        return cps

    y_cps = width_reduce(0, dout, wdn, ((1,), (1,)))

    for cp in st_cp:
        cp.wait()
    tot = stat[0]
    for k in range(1, 8):
        tot = tot + stat[k]
    mu = tot[0:1] / D
    inv = lax.rsqrt(tot[1:2] / D - mu * mu + 1e-06)
    mu8 = jnp.broadcast_to(mu, (8, T))
    inv8 = jnp.broadcast_to(inv, (8, T))
    for b in range(9):
        lanes = slice(b * 128, (b + 1) * 128)
        col[0, lanes, :] = mu8[:, lanes].T
        col[1, lanes, :] = inv8[:, lanes].T

    @pl.loop(0, 9)
    def _(b):
        rows = rows_at(b * 128, 128, 128)
        shift = dot(oh[rows, :], rmod[0])
        gain = 1.0 + dot(oh[rows, :], rmod[1])
        xh = (tok[rows, :].astype(F32) - col[0, rows, 0:1]) * col[1, rows, 0:1]
        nrm[rows, :] = (xh * gain + shift).astype(BF16)

    y_cps = y_cps + width_reduce(1, nrm, wup, ((1,), (0,)))
    for cp in y_cps:
        cp.wait()

    def width_total(a):
        v = ysum[a, y].astype(F32)
        for d in range(3):
            v = v + yrec[a, d].astype(F32)
        return v

    pre = width_total(1) + bias[...]
    sq = pre * pre
    th = jnp.tanh(ROOT * (pre + CUBE * (sq * pre)))
    mine = rows_at(c * HALF + y * CH, CH)
    had[0, mine, :] = (0.5 * pre * (1.0 + th)).astype(BF16)
    slope = 0.5 * (1.0 + th) + (0.5 * ROOT) * pre * (1.0 - th * th) * (1.0 + (3.0 * CUBE) * sq)
    had[1, mine, :] = (width_total(0) * slope).astype(BF16)

    def chunk(k, q):
        return had.at[:, rows_at(k * HALF + q * CH, CH), :]

    ya = {}
    for d in (2, 1, 3):
        ya[d] = send(chunk(c, y), chunk(c, y), ya_s.at[d - 1], ya_r.at[d - 1], at_y(d))
        ya[d].start()
    fw = [send(chunk(c, y), chunk(c, y), fw_s.at[0], fw_r.at[0], sib)]
    fw[0].start()
    for d in (1, 3, 2):
        ya[d].wait()
        src = chunk(c, (y + 4 - d) % 4)
        cp = send(src, src, fw_s.at[d], fw_r.at[d], sib)
        cp.start()
        fw.append(cp)
    for cp in fw:
        cp.wait()

    def zrows(d):
        return rows_at(((z + d) % 8) * CH, CH)

    def part(d):
        dn[zrows(d), :] = dot(had[1, zrows(d), :], wup[...], ((1,), (1,)))

    def hop(step, lanes_p, lanes_m):
        cps = []
        for k, (lanes, to) in enumerate(((lanes_p, 1), (lanes_m, 7))):
            cp = send(sb.at[k, step, :, lanes], rb.at[k, step, :, lanes], zr_s.at[k, step], zr_r.at[k, step], at_z(to))
            cp.start()
            cps.append(cp)
        return cps

    full = pl.ds(0, DW)
    part(4)
    far = dn[zrows(4), :].astype(BF16)
    sb[0, 0, :, 0:CUT] = far[:, 0:CUT]
    sb[1, 0, :, CUT:DW] = far[:, CUT:DW]
    zr = hop(0, pl.ds(0, CUT), pl.ds(CUT, DW - CUT))
    part(3)
    part(5)
    for cp in zr:
        cp.wait()
    sb[0, 1, :, 0:CUT] = (dn[zrows(3), 0:CUT] + rb[0, 0, :, 0:CUT].astype(F32)).astype(BF16)
    sb[0, 1, :, CUT:DW] = dn[zrows(3), CUT:DW].astype(BF16)
    sb[1, 1, :, 0:CUT] = dn[zrows(5), 0:CUT].astype(BF16)
    sb[1, 1, :, CUT:DW] = (dn[zrows(5), CUT:DW] + rb[1, 0, :, CUT:DW].astype(F32)).astype(BF16)
    zr = hop(1, full, full)
    part(2)
    part(6)
    part(1)
    part(7)
    part(0)
    for cp in zr:
        cp.wait()
    sb[0, 2] = (dn[zrows(2), :] + rb[0, 1].astype(F32)).astype(BF16)
    sb[1, 2] = (dn[zrows(6), :] + rb[1, 1].astype(F32)).astype(BF16)
    zr = hop(2, full, full)

    def table_block(b, carry):
        rows = rows_at(b * 128, 128, 128)
        dv = dn[rows, :]
        xh = (tok[rows, :].astype(F32) - col[0, rows, 0:1]) * col[1, rows, 0:1]
        yv = dot(had[0, rows, :], wdn[...]) * cot[rows, :].astype(F32)
        hot = oht[:, rows]
        out = []
        for acc, v in zip(carry, (dv, dv * xh, yv)):
            hi = v.astype(BF16)
            lo = (v - hi.astype(F32)).astype(BF16)
            out.append(acc + dot(hot, hi) + dot(hot, lo))
        return tuple(out)

    zero = jnp.zeros((R, DW), F32)
    sums = lax.fori_loop(0, 9, table_block, (zero, zero, zero))
    for k in range(3):
        tx[x, 2 * k] = sums[k][0:8]
        tx[x, 2 * k + 1] = sums[k][8:16]
    tcp = [send(tx.at[x], tx.at[x], tx_s.at[d - 1], tx_r.at[d - 1], at_x(d)) for d in range(1, 4)]
    for cp in tcp:
        cp.start()

    for cp in zr:
        cp.wait()
    sb[0, 3] = (dn[zrows(1), :] + rb[0, 2].astype(F32)).astype(BF16)
    sb[1, 3] = (dn[zrows(7), :] + rb[1, 2].astype(F32)).astype(BF16)
    zr = hop(3, full, full)

    for cp in tcp:
        cp.wait()
    ts[...] = (tx[0] + tx[1]) + (tx[2] + tx[3])
    for d in range(1, 8):
        @pl.when((z + d) % 8 < 6)
        def _():
            send(ts.at[(z + d) % 8], tz.at[z], tz_s.at[d - 1], tz_r.at[d - 1], at_z(d)).start()

    for m in range(4):
        n = min(128, FW - m * 128)
        gdn[m * 128 : m * 128 + n, :] = dot(had[0, :, m * 128 : m * 128 + n], dout[...], ((0,), (0,)))

    for cp in zr:
        cp.wait()
    zsum[...] = dn[zrows(0), :] + rb[0, 3].astype(F32) + rb[1, 3].astype(F32)
    for k in range(3):
        xs[k] = zsum[k * OWN : (k + 1) * OWN, :].astype(BF16)
    for d in range(1, 4):
        @pl.when((x + d) % 4 < 3)
        def _():
            send(xs.at[(x + d) % 4], xr.at[d - 1], xe_s.at[d - 1], xe_r.at[d - 1], at_x(d)).start()

    for d in range(1, 8):
        @pl.when((z + d) % 8 < 6)
        def _():
            send(ts.at[(z + d) % 8], tz.at[z], tz_s.at[d - 1], tz_r.at[d - 1], at_z(d)).wait_send()

    @pl.when(z < 6)
    def _():
        for d in range(1, 8):
            send(ts.at[0], tz.at[(z + 8 - d) % 8], tz_s.at[d - 1], tz_r.at[d - 1], at_z(d)).wait_recv()
        tz[z] = ts[z]
        v = tz[0]
        for k in range(1, 8):
            v = v + tz[k]
        tf[z] = v
        for d in range(1, 8):
            send(tf.at[z], tf.at[z], tg_s.at[d - 1], tg_r.at[d - 1], at_z(d)).start()

    for d in range(1, 4):
        @pl.when((x + d) % 4 < 3)
        def _():
            send(xs.at[(x + d) % 4], xr.at[d - 1], xe_s.at[d - 1], xe_r.at[d - 1], at_x(d)).wait_send()

    @pl.when(x < 3)
    def _():
        for d in range(1, 4):
            send(xs.at[0], xr.at[d - 1], xe_s.at[d - 1], xe_r.at[d - 1], at_x(d)).wait_recv()
        v = zsum[rows_at(x * OWN, OWN), :]
        for d in range(3):
            v = v + xr[d].astype(F32)
        rows = rows_at(z * CH + x * OWN, OWN)
        gain = 1.0 + dot(oh[rows, :], rmod[1])
        rstd = col[1, rows, 0:1]
        xh = (tok[rows, :].astype(F32) - col[0, rows, 0:1]) * rstd
        dh = v * gain
        dhx = dh * xh
        s1 = dh[:, 0:128]
        s2 = dhx[:, 0:128]
        for k in range(1, 5):
            s1 = s1 + dh[:, k * 128 : (k + 1) * 128]
            s2 = s2 + dhx[:, k * 128 : (k + 1) * 128]
        s1 = jnp.sum(s1, 1, keepdims=True)
        s2 = jnp.sum(s2, 1, keepdims=True)
        lane = lax.broadcasted_iota(jnp.int32, (OWN, 128), 1)
        mst[w] = jnp.where(lane < 64, s1, s2)
        cps = [send(mst.at[w], mst.at[w], ms_s.at[d - 1], ms_r.at[d - 1], at_w(d)) for d in range(1, 8)]
        for cp in cps:
            cp.start()
        for cp in cps:
            cp.wait()
        m = mst[0]
        for k in range(1, 8):
            m = m + mst[k]
        m = m / D
        grad = cot[rows, :].astype(F32) + rstd * (dh - m[:, 0:1] - xh * m[:, 64:65])
        gx[rows, :] = grad.astype(BF16)
        for d in range(1, 4):
            send(gx.at[rows], gx.at[rows], xg_s.at[d - 1], xg_r.at[d - 1], at_x(d)).start()
        for d in range(1, 4):
            send(gx.at[rows], gx.at[rows], xg_s.at[d - 1], xg_r.at[d - 1], at_x(d)).wait_send()

    for d in range(1, 4):
        @pl.when((x + 4 - d) % 4 < 3)
        def _():
            rows = rows_at(z * CH + ((x + 4 - d) % 4) * OWN, OWN)
            send(gx.at[rows], gx.at[rows], xg_s.at[d - 1], xg_r.at[d - 1], at_x(d)).wait_recv()

    def spread(step, lanes_p, lanes_m):
        cps = []
        for k, (lanes, to, src) in enumerate(((lanes_p, 1, 8 - step), (lanes_m, 7, step))):
            ref = gx.at[zrows(src), lanes]
            cp = send(ref, ref, zg_s.at[k, step], zg_r.at[k, step], at_z(to))
            cp.start()
            cps.append(cp)
        return cps

    zg = spread(0, full, full)

    @pl.loop(0, 5)
    def _(m):
        lanes = rows_at(m * 128, 128, 128)
        gup[lanes, :] = dot(nrm[:, lanes], had[1], ((0,), (0,)))

    gb[...] = dot(jnp.ones((8, T), BF16), had[1])[0:1]

    for cp in zg:
        cp.wait()
    zg = spread(1, full, full)

    for d in range(1, 8):
        @pl.when(z < 6)
        def _():
            send(tf.at[z], tf.at[z], tg_s.at[d - 1], tg_r.at[d - 1], at_z(d)).wait_send()

        @pl.when((z + 8 - d) % 8 < 6)
        def _():
            k = (z + 8 - d) % 8
            send(tf.at[k], tf.at[k], tg_s.at[d - 1], tg_r.at[d - 1], at_z(d)).wait_recv()

    for k in range(3):
        v = jnp.concatenate([tf[2 * k], tf[2 * k + 1]], 0)
        out = jnp.zeros((NS, DW), F32)
        for p in split3(v):
            out = out + dot(step_of, p, ((0,), (0,)))
        gtab[:, k, :] = out

    for cp in zg:
        cp.wait()
    zg = spread(2, full, full)
    for cp in zg:
        cp.wait()
    zg = spread(3, pl.ds(0, CUT), pl.ds(CUT, DW - CUT))
    for cp in zg:
        cp.wait()


def per_device(tokens, cotangent, w_up, bias_up, w_down, mod_table, seg_ids, step_ids):
    vm = pl.BlockSpec(memory_space=pltpu.VMEM)
    dma = pltpu.SemaphoreType.DMA
    outs = pl.pallas_call(
        kernel,
        out_shape=(
            jax.ShapeDtypeStruct((T, DW), BF16),
            jax.ShapeDtypeStruct((DW, FW), F32),
            jax.ShapeDtypeStruct((FW, DW), F32),
            jax.ShapeDtypeStruct((1, FW), F32),
            jax.ShapeDtypeStruct((NS, 3, DW), F32),
        ),
        in_specs=[vm] * 8,
        out_specs=(vm,) * 5,
        scratch_shapes=[
            pltpu.VMEM((8, 2, T), F32),
            pltpu.VMEM((3, 3 * R, DW), BF16),
            pltpu.VMEM((T, 3 * R), BF16),
            pltpu.VMEM((R, T), BF16),
            pltpu.VMEM((2, T, 8), F32),
            pltpu.VMEM((T, DW), BF16),
            pltpu.VMEM((T, DW), BF16),
            pltpu.VMEM((2, 4, CH, FW), BF16),
            pltpu.VMEM((2, 4, CH, FW), BF16),
            pltpu.VMEM((4, CH, FW), F32),
            pltpu.VMEM((2, 4, CH, FW), BF16),
            pltpu.VMEM((2, 3, CH, FW), BF16),
            pltpu.VMEM((2, T, FW), BF16),
            pltpu.VMEM((T, DW), F32),
            pltpu.VMEM((2, 4, CH, DW), BF16),
            pltpu.VMEM((2, 4, CH, DW), BF16),
            pltpu.VMEM((CH, DW), F32),
            pltpu.VMEM((3, OWN, DW), BF16),
            pltpu.VMEM((3, OWN, DW), BF16),
            pltpu.VMEM((8, OWN, 128), F32),
            pltpu.VMEM((8, DW), F32),
            pltpu.VMEM((4, 6, 8, DW), F32),
            pltpu.VMEM((6, 8, DW), F32),
            pltpu.VMEM((8, 8, DW), F32),
            pltpu.VMEM((6, 8, DW), F32),
            dma((7,)), dma((7,)),
            dma((2,)), dma((2,)),
            dma((2, 3)), dma((2, 3)),
            dma((3,)), dma((3,)),
            dma((4,)), dma((4,)),
            dma((2, 4)), dma((2, 4)),
            dma((3,)), dma((3,)),
            dma((7,)), dma((7,)),
            dma((3,)), dma((3,)),
            dma((2, 4)), dma((2, 4)),
            dma((3,)), dma((3,)),
            dma((7,)), dma((7,)),
            dma((7,)), dma((7,)),
        ],
        compiler_params=pltpu.CompilerParams(
            collective_id=0, has_side_effects=True, vmem_limit_bytes=56 * 1024 * 1024
        ),
        name="mlp_backward",
    )(
        tokens, cotangent, w_up, bias_up[None, :], w_down, mod_table, seg_ids[None, :], step_ids[:, None]
    )
    return outs[0], outs[1], outs[2], outs[3][0], outs[4]


def solution(mesh):
    placed = (
        P(None, "width"),
        P(None, "width"),
        P("width", "hidden"),
        P("hidden"),
        P("hidden", "width"),
        P(None, None, "width"),
        P(),
        P(),
    )
    return jax.shard_map(
        per_device,
        mesh=mesh,
        in_specs=placed,
        out_specs=(
            P(None, "width"),
            P("width", "hidden"),
            P("hidden", "width"),
            P("hidden"),
            P(None, None, "width"),
        ),
        check_vma=False,
    )
```

time: 339 us -> 128 us (0.38)
  waiting for transfers between devices: 234 us -> 0 us
  Pallas kernels: 0 us -> 112 us
  blocking collectives: 43.5 us -> 0 us
  matrix products: 29.6 us -> 0 us
  other arithmetic: 13.7 us -> 0 us
  between operations: 14.2 us -> 0.65 us
  local copies, waits for them, and re-layouts: 2.17 us -> 14.4 us
    psum x2 -> x0, waiting for transfers between devices: 234 us -> none  [the longest x1 156 us: per_device(): d_norm = lax.psum(d_part, 'hidden')]
    pallas_call x0 -> x1, Pallas kernels: none -> 112 us  [per_device(): pl.pallas_call(kernel, out_shape=(jax.ShapeDtypeStruct((T, DW), BF16), ja...]
    psum x2 -> x0, blocking collectives: 43.5 us -> none  [the longest x1 22.8 us: per_device(): lax.psum((jnp.sum(x_full, 1), jnp.sum(x_full * x_full, 1)), 'width')]
    dot_general x14 -> x0, matrix products: 29.6 us -> none  [the longest x1 3.85 us: per_device(): down_part = jnp.dot(d_out, w_down.T, preferred_element_type=jnp.float32)]
    unnamed x44 -> x13, local copies, waits for them, and re-layouts: 2.17 us -> 11.8 us
    reduce_sum x3 -> x0, other arithmetic: 9.48 us -> none  [the longest x1 5.31 us: norm_back(): jnp.sum(d_hat, 1)]
    convert_element_type x1 -> x0, other arithmetic: 3.5 us -> none  [norm_back(): return grad_rows.astype(jnp.bfloat16)]
  transfers between devices with their start and end apart: 2 -> 0, of which waited for: 2 -> 0; matrix products, arithmetic and copies ran while one was open for 1% -> 0% of each run, Pallas kernels for 0% -> 0%
where the time goes in v1:
time: 128 us; the launch traced here: 127 us
  Pallas kernels  112 us (88%)
  local copies, waits for them, and re-layouts  14.4 us (11%)
    pallas_call x1, Pallas kernels, per_device(): pl.pallas_call(kernel, out_shape=(jax.ShapeDtypeStruct((T, DW), BF16), ja...  112 us
    unnamed x13, local copies, waits for them, and re-layouts  11.8 us

profile of v1, /device:TPU:8, one launch (start us, length us, event | category | flops | bytes accessed | tf_op | source)
XLA Modules:
  0.0 127.3 jit_solution(14766091913824287634)
XLA Ops:
  0.6 1.3 %broadcast_in_dim.10.seg = s32[1,1152]{1,0:T(1,128)} reshape(s32[1152]{0:T(1024)} %param.14) | data formatting | bytes 9216 | tf_op jit(solution)/shard_map/broadcast_in_dim | solution.py:469
  1.9 1.3 %copy.15.stp = s32[16,1]{1,0:T(8,128)} copy(s32[16,1]{0,1:T(1,128)} %bitcast.5) | data formatting | bytes 128 | tf_op jit(solution)/shard_map/broadcast_in_dim | solution.py:469
  3.3 1.8 %copy.14.tab = f32[32,3,640]{2,1,0:T(4,128)} copy(f32[32,3,640]{2,0,1:T(8,128)} %param.13) | data formatting | bytes 491520 | tf_op args[5]
  5.1 2.1 %copy.13.wup = bf16[640,432]{1,0:T(8,128)(2,1)} copy(bf16[640,432]{0,1:T(8,128)(2,1)} %param.10) | data formatting | bytes 1105920 | tf_op args[2]
  7.2 112.2 %mlp_backward.1 = (bf16[1152,640]{1,0:T(8,128)(2,1)}, f32[640,432]{1,0:T(8,128)}, f32[432,640]{1,0:T(8,128)}, f32[1,432]{1,0:T(1,128)}, f32[32,3,640]{2,1,0:T(4,128)}) custom-call(bf16[1152,640]{1,0:T(8,128)(2,1)} %tok.1, bf16[1152,640]{1,0:T(8,128)(2,1)} %cot.1, bf16[640,432]{1,0:T(8,128)(2,1)} %copy.13.wup, f32[1,432]{1,0:T(1,128)} %bitcast.3, ...), custom_call_target="tpu_custom_call" | custom-call | tf_op jit(solution)/shard_map/mlp_backward/pallas_call | solution.py:413
  119.4 0.0 copy-start
  119.4 1.8 %copy.17 = f32[32,3,640]{2,0,1:T(8,128)} copy(f32[32,3,640]{2,1,0:T(4,128)} %get-tuple-element.19) | data formatting | bytes 491520
  121.2 2.7 %copy.16 = f32[640,432]{0,1:T(8,128)} copy(f32[640,432]{1,0:T(8,128)} %get-tuple-element.16) | data formatting | bytes 2211840
  123.9 0.0 copy-done
  123.9 0.0 copy-start.1
  123.9 1.1 copy.21
  125.0 0.7 copy-done.1
  125.7 0.0 copy-start.2
  125.7 1.0 copy.22
  126.7 0.0 copy-done.2
  126.7 0.6 copy.23
Async XLA Ops:
  119.4 4.5 %copy-start = (bf16[1152,640]{1,0:T(8,128)(2,1)S(1)}, bf16[1152,640]{1,0:T(8,128)(2,1)}, u32[]{:S(2)}) copy-start(bf16[1152,640]{1,0:T(8,128)(2,1)} %get-tuple-element.25) | copy-start | bytes 4423684
  123.9 1.8 %copy-start.1 = (f32[432,640]{1,0:T(8,128)S(1)}, f32[432,640]{1,0:T(8,128)}, u32[]{:S(2)}) copy-start(f32[432,640]{1,0:T(8,128)} %get-tuple-element.27) | copy-start | bytes 3317764
  125.7 1.0 copy-start.2

commit v2 on v0

v2 whole, which is shorter than its diff:
```python
import functools

import jax
import jax.numpy as jnp
from jax import lax
from jax.experimental import pallas as pl
from jax.experimental.pallas import tpu as pltpu
from jax.sharding import PartitionSpec as P

MESH = pl.DeviceIdType.MESH
F32, BF16 = jnp.float32, jnp.bfloat16

T, DW, FW, R, NS = 1152, 640, 432, 16, 32
D = 5120
NB = 3
BLK = 384
OWN = 48
HALF = 192
CUT = 384
ROOT = 0.7978845608028654
CUBE = 0.044715


def split3(v):
    hi = v.astype(BF16)
    rest = v - hi.astype(F32)
    mid = rest.astype(BF16)
    return hi, mid, (rest - mid.astype(F32)).astype(BF16)


def dot(a, b, dims=((1,), (0,))):
    return lax.dot_general(a, b, (dims, ((), ())), preferred_element_type=F32)


def rows_at(start, size, step=16):
    return pl.ds(pl.multiple_of(start, step), size)


def kernel(
    tok_h, cot_h, wup_h, bias, wdn_h, tab, seg, stp,
    gx, gup_h, gdn_h, gb, gtab,
    tok, cot, wup, wdn, gup, gdn,
    stat, rmod, oh, oht, col, dout, nrm,
    psib, rsib, pown, ysum, yrec, had,
    dn, sb, rb, zsum, xs, xr, dhv, mst,
    tx, tz, tf, comp,
    in_s, out_s, st_s, st_r, cx_s, cx_r, yd_s, yd_r, yu_s, yu_r, ya_s, ya_r, fw_s, fw_r,
    ha_s, ha_r, hf_s, hf_r, zr_s, zr_r, xe_s, xe_r, ms_s, ms_r, xg_s, xg_r, zg_s, zg_r,
    tx_s, tx_r, tz_s, tz_r, tg_s, tg_r, tb_s, tb_r,
):
    w = lax.axis_index("width")
    h = lax.axis_index("hidden")
    y, c = w // 2, w % 2
    z, x = h // 4, h % 4
    me = c * 4 + y

    def at_w(d):
        return ((w + d) % 8, h)

    def at_y(d):
        return (((y + d) % 4) * 2 + c, h)

    sib = (y * 2 + 1 - c, h)

    def at_z(d):
        return (w, ((z + d) % 8) * 4 + x)

    def at_x(d):
        return (w, z * 4 + (x + d) % 4)

    def send(src, dst, s_sem, r_sem, dev):
        return pltpu.make_async_remote_copy(
            src_ref=src, dst_ref=dst, send_sem=s_sem, recv_sem=r_sem, device_id=dev, device_id_type=MESH
        )

    loads = {}
    for i, (name, src, dst) in enumerate(
        (("tok", tok_h, tok), ("cot", cot_h, cot), ("wdn", wdn_h, wdn), ("wup", wup_h, wup))
    ):
        loads[name] = pltpu.make_async_copy(src, dst, in_s.at[i])
        loads[name].start()

    bar = pltpu.get_barrier_semaphore()
    for d in range(1, 8):
        pl.semaphore_signal(bar, inc=1, device_id=at_w(d), device_id_type=MESH)
        pl.semaphore_signal(bar, inc=1, device_id=at_z(d), device_id_type=MESH)
    for d in range(1, 4):
        pl.semaphore_signal(bar, inc=1, device_id=at_x(d), device_id_type=MESH)

    row = lax.broadcasted_iota(jnp.int32, (R, NS), 0)
    picked = jnp.zeros((R, NS), jnp.int32)
    for r in range(R):
        picked = jnp.where(row == r, stp[r], picked)
    step_of = (picked == lax.broadcasted_iota(jnp.int32, (R, NS), 1)).astype(F32).astype(BF16)
    for k in range(3):
        parts = split3(tab[k])
        rm = dot(step_of, parts[0]) + dot(step_of, parts[1]) + dot(step_of, parts[2])
        for i, part in enumerate(split3(rm)):
            rmod[k, i * R : (i + 1) * R, :] = part

    loads["tok"].wait()

    @pl.loop(0, 9)
    def _(b):
        v = tok[rows_at(b * 128, 128, 128), :].astype(F32)
        s1 = v[:, 0:128]
        s2 = v[:, 0:128] * v[:, 0:128]
        for k in range(1, 5):
            p = v[:, k * 128 : (k + 1) * 128]
            s1 = s1 + p
            s2 = s2 + p * p
        lanes = rows_at(b * 128, 128, 128)
        stat[w, 0:1, lanes] = jnp.sum(s1.T, 0, keepdims=True)
        stat[w, 1:2, lanes] = jnp.sum(s2.T, 0, keepdims=True)

    pl.semaphore_wait(bar, 17)

    st_cp = [send(stat.at[w], stat.at[w], st_s.at[d - 1], st_r.at[d - 1], at_w(d)) for d in range(1, 8)]
    for cp in st_cp:
        cp.start()

    loads["cot"].wait()

    @pl.loop(0, 9)
    def _(b):
        lanes = rows_at(b * 128, 128, 128)
        ids = jnp.broadcast_to(seg[lanes].reshape(1, 128), (R, 128))
        one = (ids == lax.broadcasted_iota(jnp.int32, (R, 128), 0)).astype(F32)
        oht[:, lanes] = one.astype(BF16)
        three = jnp.concatenate([one, one, one], 0)
        oh[lanes, :] = three.T.astype(BF16)
        gate = dot(oh[lanes, :], rmod[2])
        dout[lanes, :] = (cot[lanes, :].astype(F32) * gate).astype(BF16)

    def pair_sum(a, left, right):
        @pl.loop(0, NB)
        def _(b):
            p = dot(left[rows_at(b * BLK + (1 - c) * HALF, HALF), :], right[...], ((1,), (1,))).astype(BF16)
            for k in range(4):
                psib[a, b, k] = p[k * OWN : (k + 1) * OWN]

        cx = send(psib.at[a], rsib.at[a], cx_s.at[a], cx_r.at[a], sib)
        cx.start()

        @pl.loop(0, NB)
        def _(b):
            p = dot(left[rows_at(b * BLK + c * HALF, HALF), :], right[...], ((1,), (1,)))
            for k in range(4):
                pown[b, k] = p[k * OWN : (k + 1) * OWN]

        cx.wait()

        @pl.loop(0, NB)
        def _(b):
            for k in range(4):
                ysum[a, k, b] = (pown[b, k] + rsib[a, b, k].astype(F32)).astype(BF16)

    loads["wdn"].wait()
    pair_sum(0, dout, wdn)
    yd = []
    for d in (2, 1, 3):
        yd.append(send(ysum.at[0, (y + d) % 4], yrec.at[0, d - 1], yd_s.at[d - 1], yd_r.at[d - 1], at_y(d)))
        yd[-1].start()

    for cp in st_cp:
        cp.wait()
    tot = stat[0]
    for k in range(1, 8):
        tot = tot + stat[k]
    mu = tot[0:1] / D
    inv = lax.rsqrt(tot[1:2] / D - mu * mu + 1e-06)
    mu8 = jnp.broadcast_to(mu, (8, T))
    inv8 = jnp.broadcast_to(inv, (8, T))
    for b in range(9):
        lanes = slice(b * 128, (b + 1) * 128)
        col[0, lanes, :] = mu8[:, lanes].T
        col[1, lanes, :] = inv8[:, lanes].T

    @pl.loop(0, 9)
    def _(b):
        rows = rows_at(b * 128, 128, 128)
        shift = dot(oh[rows, :], rmod[0])
        gain = 1.0 + dot(oh[rows, :], rmod[1])
        xh = (tok[rows, :].astype(F32) - col[0, rows, 0:1]) * col[1, rows, 0:1]
        nrm[rows, :] = (xh * gain + shift).astype(BF16)

    loads["wup"].wait()
    pair_sum(1, nrm, wup)
    yu = {}
    for b in range(NB):
        for d in (2, 1, 3):
            yu[b, d] = send(
                ysum.at[1, (y + d) % 4, b], yrec.at[1, d - 1, b], yu_s.at[b, d - 1], yu_r.at[b, d - 1], at_y(d)
            )
            yu[b, d].start()
    for cp in yd:
        cp.wait()

    def total(a, b):
        v = ysum[a, y, b].astype(F32)
        for d in range(3):
            v = v + yrec[a, d, b].astype(F32)
        return v

    def own(kind, b, k, q):
        return had.at[kind, b, rows_at(k * HALF + q * OWN, OWN), :]

    ya, fw = {}, {}
    for b in range(NB):
        for d in (1, 2, 3):
            yu[b, d].wait()
        pre = total(1, b) + bias[...]
        sq = pre * pre
        th = jnp.tanh(ROOT * (pre + CUBE * (sq * pre)))
        slope = 0.5 * (1.0 + th) + (0.5 * ROOT) * pre * (1.0 - th * th) * (1.0 + (3.0 * CUBE) * sq)
        mine = rows_at(me * OWN, OWN)
        had[1, b, mine, :] = (total(0, b) * slope).astype(BF16)
        had[0, b, mine, :] = (0.5 * pre * (1.0 + th)).astype(BF16)
        src = own(1, b, c, y)
        for d in (2, 1, 3):
            ya[b, d] = send(src, src, ya_s.at[b, d - 1], ya_r.at[b, d - 1], at_y(d))
            ya[b, d].start()
        fw[b, 0] = send(src, src, fw_s.at[b, 0], fw_r.at[b, 0], sib)
        fw[b, 0].start()

    def own3(k, q):
        return had.at[0, :, rows_at(k * HALF + q * OWN, OWN), :]

    ha, hf = {}, {}
    for d in (2, 1, 3):
        ha[d] = send(own3(c, y), own3(c, y), ha_s.at[d - 1], ha_r.at[d - 1], at_y(d))
        ha[d].start()
    hf[0] = send(own3(c, y), own3(c, y), hf_s.at[0], hf_r.at[0], sib)
    hf[0].start()

    def zrow(b, d):
        return rows_at(b * BLK + ((z + d) % 8) * OWN, OWN)

    def gather(b):
        for d in (1, 3, 2):
            ya[b, d].wait()
            src = own(1, b, c, (y + 4 - d) % 4)
            fw[b, d] = send(src, src, fw_s.at[b, d], fw_r.at[b, d], sib)
            fw[b, d].start()
        for d in range(4):
            fw[b, d].wait()
        dn[b * BLK : (b + 1) * BLK, :] = dot(had[1, b], wup[...])

    zr = {}

    def hop(b, s):
        if s == 0:
            far = dn[zrow(b, 4), :].astype(BF16)
            sb[b, 0, 0, :, 0:CUT] = far[:, 0:CUT]
            sb[b, 1, 0, :, CUT:DW] = far[:, CUT:DW]
        else:
            for cp in zr[b, s - 1]:
                cp.wait()
            if s == 1:
                sb[b, 0, 1, :, 0:CUT] = (dn[zrow(b, 3), 0:CUT] + rb[b, 0, 0, :, 0:CUT].astype(F32)).astype(BF16)
                sb[b, 0, 1, :, CUT:DW] = dn[zrow(b, 3), CUT:DW].astype(BF16)
                sb[b, 1, 1, :, 0:CUT] = dn[zrow(b, 5), 0:CUT].astype(BF16)
                sb[b, 1, 1, :, CUT:DW] = (dn[zrow(b, 5), CUT:DW] + rb[b, 1, 0, :, CUT:DW].astype(F32)).astype(BF16)
            else:
                sb[b, 0, s] = (dn[zrow(b, 4 - s), :] + rb[b, 0, s - 1].astype(F32)).astype(BF16)
                sb[b, 1, s] = (dn[zrow(b, 4 + s), :] + rb[b, 1, s - 1].astype(F32)).astype(BF16)
        zr[b, s] = []
        for k, to in ((0, 1), (1, 7)):
            lanes = pl.ds(0, DW)
            if s == 0:
                lanes = pl.ds(k * CUT, CUT if k == 0 else DW - CUT)
            cp = send(
                sb.at[b, k, s, :, lanes], rb.at[b, k, s, :, lanes], zr_s.at[b, k, s], zr_r.at[b, k, s], at_z(to)
            )
            cp.start()
            zr[b, s].append(cp)

    def reach(b):
        return send(
            xs.at[b], xr.at[(x + 3 - b) % 4], xe_s.at[b], xe_r.at[(x + 3 - b) % 4], (w, z * 4 + b)
        )

    def land(b):
        for cp in zr[b, 3]:
            cp.wait()
        v = dn[zrow(b, 0), :] + rb[b, 0, 3].astype(F32) + rb[b, 1, 3].astype(F32)

        @pl.when(x == b)
        def _():
            zsum[...] = v

        @pl.when(x != b)
        def _():
            xs[b] = v.astype(BF16)
            reach(b).start()

    def table_block(b, carry):
        rows = rows_at(b * 128, 128, 128)
        dv = dn[rows, :]
        xh = (tok[rows, :].astype(F32) - col[0, rows, 0:1]) * col[1, rows, 0:1]
        hid = had[0, b // 3, rows_at((b % 3) * 128, 128, 128), :]
        yv = dot(hid, wdn[...]) * cot[rows, :].astype(F32)
        hot = oht[:, rows]
        out = []
        for acc, v in zip(carry, (dv, dv * xh, yv)):
            hi = v.astype(BF16)
            lo = (v - hi.astype(F32)).astype(BF16)
            out.append(acc + dot(hot, hi) + dot(hot, lo))
        return tuple(out)

    gather(0)
    hop(0, 0)
    gather(1)
    hop(1, 0)
    hop(0, 1)
    gather(2)
    hop(2, 0)
    hop(1, 1)
    hop(0, 2)
    for d in (1, 3, 2):
        ha[d].wait()
        src = own3(c, (y + 4 - d) % 4)
        hf[d] = send(src, src, hf_s.at[d], hf_r.at[d], sib)
        hf[d].start()
    hop(2, 1)
    hop(1, 2)
    hop(0, 3)
    for d in range(4):
        hf[d].wait()
    zero = jnp.zeros((R, DW), F32)
    sums = lax.fori_loop(0, 3, table_block, (zero, zero, zero))
    hop(2, 2)
    hop(1, 3)
    land(0)
    sums = lax.fori_loop(3, 6, table_block, sums)
    hop(2, 3)
    land(1)
    sums = lax.fori_loop(6, 9, table_block, sums)

    for k in range(3):
        for q in range(8):
            tx[k, 3, q] = sums[k][2 * q : 2 * q + 2]

    def kind_out(k):
        return send(
            tx.at[k, 3], tx.at[k, (x + 3 - k) % 4], tx_s.at[k], tx_r.at[(x + 3 - k) % 4], (w, z * 4 + k)
        )

    for k in range(3):
        @pl.when(x != k)
        def _():
            kind_out(k).start()

    def modul(b):
        rows = zrow(b, 0)
        gain = 1.0 + dot(oh[rows, :], rmod[1])
        rstd = col[1, rows, 0:1]
        xh = (tok[rows, :].astype(F32) - col[0, rows, 0:1]) * rstd
        return rows, gain, rstd, xh

    def ms_copies():
        return [send(mst.at[w], mst.at[w], ms_s.at[d - 1], ms_r.at[d - 1], at_w(d)) for d in range(1, 8)]

    def finish_sums(b):
        @pl.when(x == b)
        def _():
            for d in range(3):
                send(xs.at[0], xr.at[d], xe_s.at[0], xe_r.at[d], at_x(1)).wait_recv()
            v = zsum[...]
            for d in range(3):
                v = v + xr[d].astype(F32)
            rows, gain, rstd, xh = modul(b)
            dh = v * gain
            dhv[...] = dh
            dhx = dh * xh
            s1 = dh[:, 0:128]
            s2 = dhx[:, 0:128]
            for k in range(1, 5):
                s1 = s1 + dh[:, k * 128 : (k + 1) * 128]
                s2 = s2 + dhx[:, k * 128 : (k + 1) * 128]
            both = jnp.concatenate([s1, s2, jnp.zeros((128 - 2 * OWN, 128), F32)], 0)
            mst[w] = jnp.sum(both.T, 0, keepdims=True)
            for cp in ms_copies():
                cp.start()

    def give(b, d):
        rows = zrow(b, 0)
        return send(gx.at[rows], gx.at[rows], xg_s.at[d - 1], xg_r.at[b], at_x(d))

    def finish_rows(b):
        @pl.when(x == b)
        def _():
            for cp in ms_copies():
                cp.wait()
            m = mst[0]
            for k in range(1, 8):
                m = m + mst[k]
            mt = jnp.broadcast_to(m / D, (8, 128)).T
            rows, _, rstd, xh = modul(b)
            grad = cot[rows, :].astype(F32) + rstd * (dhv[...] - mt[0:OWN, 0:1] - xh * mt[OWN : 2 * OWN, 0:1])
            gx[rows, :] = grad.astype(BF16)
            for d in (2, 1, 3):
                give(b, d).start()

    finish_sums(0)
    land(2)
    finish_sums(1)
    finish_rows(0)
    finish_sums(2)
    finish_rows(1)
    finish_rows(2)

    zg = {}

    def spread(b, s):
        if s == 0:
            @pl.when(x != b)
            def _():
                give(b, 1).wait_recv()
        else:
            for cp in zg[b, s - 1]:
                cp.wait()
        if s < 4:
            zg[b, s] = []
            for k, (to, src) in enumerate(((1, 8 - s), (7, s))):
                lanes = pl.ds(0, DW)
                if s == 3:
                    lanes = pl.ds(k * CUT, CUT if k == 0 else DW - CUT)
                ref = gx.at[zrow(b, src), lanes]
                cp = send(ref, ref, zg_s.at[b, k, s], zg_r.at[b, k, s], at_z(to))
                cp.start()
                zg[b, s].append(cp)

    spread(0, 0)
    spread(1, 0)

    @pl.when(x < 3)
    def _():
        for d in range(3):
            send(tx.at[0, 3], tx.at[0, d], tx_s.at[0], tx_r.at[d], at_x(1)).wait_recv()
        tz[8] = (tx[x, 0] + tx[x, 1]) + (tx[x, 2] + tx[x, 3])
        for d in range(1, 8):
            send(tz.at[8, (z + d) % 8], tz.at[z, 0], tz_s.at[d - 1], tz_r.at[d - 1], at_z(d)).start()

    spread(0, 1)
    spread(2, 0)

    @pl.when(x < 3)
    def _():
        for d in range(1, 8):
            send(tz.at[8, 0], tz.at[0, 0], tz_s.at[d - 1], tz_r.at[d - 1], at_z(d)).wait()
        tz[z, 0] = tz[8, z]
        v = tz[0, 0]
        for k in range(1, 8):
            v = v + tz[k, 0]
        tf[x, z] = v
        for d in range(1, 8):
            send(tf.at[x, z], tf.at[x, z], tg_s.at[d - 1], tg_r.at[d - 1], at_z(d)).start()

    spread(1, 1)
    spread(0, 2)
    spread(2, 1)

    @pl.when(x < 3)
    def _():
        for d in range(1, 8):
            send(tf.at[x, z], tf.at[x, z], tg_s.at[d - 1], tg_r.at[d - 1], at_z(d)).wait()
        for d in range(1, 4):
            send(tf.at[x], tf.at[x], tb_s.at[d - 1], tb_r.at[x], at_x(d)).start()

    spread(1, 2)
    spread(0, 3)

    hid = had[0].reshape(T, FW)
    for m in range(4):
        n = min(128, FW - m * 128)
        gdn[m * 128 : m * 128 + n, :] = dot(hid[:, m * 128 : m * 128 + n], dout[...], ((0,), (0,)))
    out0 = pltpu.make_async_copy(gdn, gdn_h, out_s.at[0])
    out0.start()
    spread(2, 2)
    spread(1, 3)
    pre_g = had[1].reshape(T, FW)
    for m in range(4):
        n = min(128, FW - m * 128)
        gup[m * 128 : m * 128 + n, :] = dot(pre_g[:, m * 128 : m * 128 + n], nrm[...], ((0,), (0,)))
    out1 = pltpu.make_async_copy(gup, gup_h, out_s.at[1])
    out1.start()
    gb[...] = dot(jnp.ones((8, T), BF16), pre_g)[0:1]
    spread(2, 3)

    for k in range(3):
        @pl.when(x != k)
        def _():
            send(tf.at[k], tf.at[k], tb_s.at[0], tb_r.at[k], at_x(1)).wait_recv()
            kind_out(k).wait_send()
            reach(k).wait_send()

        @pl.when(x == k)
        def _():
            for d in range(1, 4):
                send(tf.at[k], tf.at[k], tb_s.at[d - 1], tb_r.at[k], at_x(d)).wait_send()
                give(k, d).wait_send()

    for k in range(3):
        for q in range(8):
            comp[k, 2 * q : 2 * q + 2, :] = tf[k, q]
        out = jnp.zeros((NS, DW), F32)
        for p in split3(comp[k]):
            out = out + dot(step_of, p, ((0,), (0,)))
        gtab[k] = out

    for b in range(NB):
        spread(b, 4)
    out0.wait()
    out1.wait()


def per_device(tokens, cotangent, w_up, bias_up, w_down, mod_table, seg_ids, step_ids):
    vm = pl.BlockSpec(memory_space=pltpu.VMEM)
    sm = pl.BlockSpec(memory_space=pltpu.SMEM)
    hbm = pl.BlockSpec(memory_space=pl.ANY)
    dma = pltpu.SemaphoreType.DMA
    outs = pl.pallas_call(
        kernel,
        out_shape=(
            jax.ShapeDtypeStruct((T, DW), BF16),
            jax.ShapeDtypeStruct((FW, DW), F32),
            jax.ShapeDtypeStruct((FW, DW), F32),
            jax.ShapeDtypeStruct((1, FW), F32),
            jax.ShapeDtypeStruct((3, NS, DW), F32),
        ),
        in_specs=[hbm, hbm, hbm, vm, hbm, vm, vm, sm],
        out_specs=(vm, hbm, hbm, vm, vm),
        scratch_shapes=[
            pltpu.VMEM((T, DW), BF16),
            pltpu.VMEM((T, DW), BF16),
            pltpu.VMEM((FW, DW), BF16),
            pltpu.VMEM((FW, DW), BF16),
            pltpu.VMEM((FW, DW), F32),
            pltpu.VMEM((FW, DW), F32),
            pltpu.VMEM((8, 2, T), F32),
            pltpu.VMEM((3, 3 * R, DW), BF16),
            pltpu.VMEM((T, 3 * R), BF16),
            pltpu.VMEM((R, T), BF16),
            pltpu.VMEM((2, T, 8), F32),
            pltpu.VMEM((T, DW), BF16),
            pltpu.VMEM((T, DW), BF16),
            pltpu.VMEM((2, NB, 4, OWN, FW), BF16),
            pltpu.VMEM((2, NB, 4, OWN, FW), BF16),
            pltpu.VMEM((NB, 4, OWN, FW), F32),
            pltpu.VMEM((2, 4, NB, OWN, FW), BF16),
            pltpu.VMEM((2, 3, NB, OWN, FW), BF16),
            pltpu.VMEM((2, NB, BLK, FW), BF16),
            pltpu.VMEM((T, DW), F32),
            pltpu.VMEM((NB, 2, 4, OWN, DW), BF16),
            pltpu.VMEM((NB, 2, 4, OWN, DW), BF16),
            pltpu.VMEM((OWN, DW), F32),
            pltpu.VMEM((NB, OWN, DW), BF16),
            pltpu.VMEM((3, OWN, DW), BF16),
            pltpu.VMEM((OWN, DW), F32),
            pltpu.VMEM((8, 1, 128), F32),
            pltpu.VMEM((3, 4, 8, 2, DW), F32),
            pltpu.VMEM((9, 8, 2, DW), F32),
            pltpu.VMEM((3, 8, 2, DW), F32),
            pltpu.VMEM((3, R, DW), F32),
            dma((4,)), dma((2,)),
            dma((7,)), dma((7,)),
            dma((2,)), dma((2,)),
            dma((3,)), dma((3,)),
            dma((NB, 3)), dma((NB, 3)),
            dma((NB, 3)), dma((NB, 3)),
            dma((NB, 4)), dma((NB, 4)),
            dma((3,)), dma((3,)),
            dma((4,)), dma((4,)),
            dma((NB, 2, 4)), dma((NB, 2, 4)),
            dma((NB,)), dma((3,)),
            dma((7,)), dma((7,)),
            dma((3,)), dma((NB,)),
            dma((NB, 2, 4)), dma((NB, 2, 4)),
            dma((3,)), dma((3,)),
            dma((7,)), dma((7,)),
            dma((7,)), dma((7,)),
            dma((3,)), dma((3,)),
        ],
        compiler_params=pltpu.CompilerParams(
            collective_id=0, has_side_effects=True, vmem_limit_bytes=56 * 1024 * 1024
        ),
        name="mlp_backward",
    )(
        tokens, cotangent, w_up.T, bias_up[None, :], w_down, mod_table.transpose(1, 0, 2), seg_ids, step_ids
    )
    return outs[0], outs[1].T, outs[2], outs[3][0], outs[4].transpose(1, 0, 2)


def solution(mesh):
    placed = (
        P(None, "width"),
        P(None, "width"),
        P("width", "hidden"),
        P("hidden"),
        P("hidden", "width"),
        P(None, None, "width"),
        P(),
        P(),
    )
    return jax.shard_map(
        per_device,
        mesh=mesh,
        in_specs=placed,
        out_specs=(
            P(None, "width"),
            P("width", "hidden"),
            P("hidden", "width"),
            P("hidden"),
            P(None, None, "width"),
        ),
        check_vma=False,
    )
```

time: 339 us -> 98.5 us (0.29)
  waiting for transfers between devices: 234 us -> 0 us
  Pallas kernels: 0 us -> 90.8 us
  blocking collectives: 43.5 us -> 0 us
  matrix products: 29.6 us -> 0 us
  other arithmetic: 13.7 us -> 0 us
  between operations: 14.2 us -> 0.66 us
  local copies, waits for them, and re-layouts: 2.17 us -> 6.62 us
    psum x2 -> x0, waiting for transfers between devices: 234 us -> none  [the longest x1 156 us: per_device(): d_norm = lax.psum(d_part, 'hidden')]
    pallas_call x0 -> x1, Pallas kernels: none -> 90.8 us  [per_device(): pl.pallas_call(kernel, out_shape=(jax.ShapeDtypeStruct((T, DW), BF16), ja...]
    psum x2 -> x0, blocking collectives: 43.5 us -> none  [the longest x1 22.8 us: per_device(): lax.psum((jnp.sum(x_full, 1), jnp.sum(x_full * x_full, 1)), 'width')]
    dot_general x14 -> x0, matrix products: 29.6 us -> none  [the longest x1 3.85 us: per_device(): down_part = jnp.dot(d_out, w_down.T, preferred_element_type=jnp.float32)]
    reduce_sum x3 -> x0, other arithmetic: 9.48 us -> none  [the longest x1 5.31 us: norm_back(): jnp.sum(d_hat, 1)]
    unnamed x44 -> x13, local copies, waits for them, and re-layouts: 2.17 us -> 6.62 us
    convert_element_type x1 -> x0, other arithmetic: 3.5 us -> none  [norm_back(): return grad_rows.astype(jnp.bfloat16)]
  transfers between devices with their start and end apart: 2 -> 0, of which waited for: 2 -> 0; matrix products, arithmetic and copies ran while one was open for 1% -> 0% of each run, Pallas kernels for 0% -> 0%
where the time goes in v2:
time: 98.5 us; the launch traced here: 98.1 us
  Pallas kernels  90.8 us (92%)
  local copies, waits for them, and re-layouts  6.62 us (7%)
    pallas_call x1, Pallas kernels, per_device(): pl.pallas_call(kernel, out_shape=(jax.ShapeDtypeStruct((T, DW), BF16), ja...  90.8 us
    unnamed x13, local copies, waits for them, and re-layouts  6.62 us

profile of v2, /device:TPU:8, one launch (start us, length us, event | category | flops | bytes accessed | tf_op | source)
XLA Modules:
  0.0 98.1 jit_solution(6152526737904910487)
XLA Ops:
  0.6 90.8 %mlp_backward.1 = (bf16[1152,640]{1,0:T(8,128)(2,1)}, f32[432,640]{1,0:T(8,128)}, f32[432,640]{1,0:T(8,128)}, f32[1,432]{1,0:T(1,128)}, f32[3,32,640]{2,1,0:T(8,128)}) custom-call(bf16[1152,640]{1,0:T(8,128)(2,1)} %tok_h.1, bf16[1152,640]{1,0:T(8,128)(2,1)} %cot_h.1, bf16[432,640]{1,0:T(8,128)(2,1)} %bitcast.7, f32[1,432]{1,0:T(1,128)} %bitcast.10, ...), custom_call_target="tpu_custom_call" | custom-call | tf_op jit(solution)/shard_map/mlp_backward/pallas_call | solution.py:523
  91.5 0.0 copy-start.1
  91.5 2.7 %copy.18 = bf16[1152,640]{1,0:T(8,128)(2,1)} copy(bf16[1152,640]{1,0:T(8,128)(2,1)} %get-tuple-element.20) | data formatting | bytes 2949120
  94.2 0.0 copy-done.1
  94.2 0.0 copy-start
  94.2 1.0 %copy.19 = f32[640,432]{0,1:T(8,128)} copy(f32[640,432]{0,1:T(8,128)S(1)} %bitcast.6) | data formatting | bytes 2211840
  95.2 0.7 copy-done
  95.8 0.0 copy-start.3
  95.8 0.0 copy-start.2
  95.8 1.0 %copy.20 = f32[432,640]{1,0:T(8,128)} copy(f32[432,640]{1,0:T(8,128)S(1)} %copy-done) | data formatting | bytes 2211840
  96.8 0.0 copy-done.3
  96.8 0.6 copy.21
  97.4 0.0 copy-done.2
  97.4 0.7 copy.22
Async XLA Ops:
  91.5 2.7 %copy-start.1 = (f32[432,640]{1,0:T(8,128)S(1)}, f32[432,640]{1,0:T(8,128)}, u32[]{:S(2)}) copy-start(f32[432,640]{1,0:T(8,128)} %get-tuple-element.11) | copy-start | bytes 3317764
  94.2 1.6 %copy-start = (f32[432,640]{1,0:T(8,128)S(1)}, f32[432,640]{1,0:T(8,128)}, u32[]{:S(2)}) copy-start(f32[432,640]{1,0:T(8,128)} %get-tuple-element.22) | copy-start | bytes 3317764
  95.8 1.0 %copy-start.3 = (f32[1,432]{1,0:T(1,128)S(1)}, f32[1,432]{1,0:T(1,128)}, u32[]{:S(2)}) copy-start(f32[1,432]{1,0:T(1,128)} %get-tuple-element.13) | copy-start | bytes 5188
  95.8 1.6 %copy-start.2 = (f32[3,32,640]{2,1,0:T(8,128)S(1)}, f32[3,32,640]{2,1,0:T(8,128)}, u32[]{:S(2)}) copy-start(f32[3,32,640]{2,1,0:T(8,128)} %get-tuple-element.14) | copy-start | bytes 737284

commit v3 on v0

v3 whole, which is shorter than its diff:
```python
import functools

import jax
import jax.numpy as jnp
from jax import lax
from jax.experimental import pallas as pl
from jax.experimental.pallas import tpu as pltpu
from jax.sharding import PartitionSpec as P

MESH = pl.DeviceIdType.MESH
F32, BF16 = jnp.float32, jnp.bfloat16

T, DW, FW, R, NS = 1152, 640, 432, 16, 32
D = 5120
UNITS = (3, 3, 3)
NB = len(UNITS)
OB = tuple(16 * u for u in UNITS)
OFF = tuple(sum(OB[:b]) for b in range(NB))
CH = sum(OB)
CUT = 384
YCUT = 256
ROOT = 0.7978845608028654
CUBE = 0.044715


def split3(v):
    hi = v.astype(BF16)
    rest = v - hi.astype(F32)
    mid = rest.astype(BF16)
    return hi, mid, (rest - mid.astype(F32)).astype(BF16)


def dot(a, b, dims=((1,), (0,))):
    return lax.dot_general(a, b, (dims, ((), ())), preferred_element_type=F32)


def rows_at(start, size, step=16):
    return pl.ds(pl.multiple_of(start, step), size)


def kernel(
    tok_h, cot_h, wup_h, bias_h, wdn_h, tab_h, seg_h, stp,
    gx, gup, gdn, gb, gtab,
    tok, cot, wup, bias, wdn, tab, seg,
    stat, rmod, oh, oht, col, dout, nrm,
    psib, rsib, pown, yo, yh, ys, yr, had,
    dn, sb, rb, xa, dhv, mst,
    tx, tz, tf, comp,
    in_s, st_s, st_r, cx_s, cx_r, y_s, yh_r, yr_r, ag_s, a1_r, a2_r, fw_r,
    zr_s, zr_r, xe_s, xe_r, ms_s, ms_r, zg_s, zg_r,
    tx_s, tx_r, tz_s, tz_r, tg_s, tg_r, tb_s, tb_r,
):
    w = lax.axis_index("width")
    h = lax.axis_index("hidden")
    y, c = w // 2, w % 2
    z, x = h // 4, h % 4

    def at_w(d):
        return ((w + d) % 8, h)

    def at_y(d):
        return (((y + d) % 4) * 2 + c, h)

    sib = (y * 2 + 1 - c, h)

    def at_z(d):
        return (w, ((z + d) % 8) * 4 + x)

    def at_x(d):
        return (w, z * 4 + (x + d) % 4)

    def send(src, dst, s_sem, r_sem, dev):
        return pltpu.make_async_remote_copy(
            src_ref=src, dst_ref=dst, send_sem=s_sem, recv_sem=r_sem, device_id=dev, device_id_type=MESH
        )

    def received(ref, sem):
        send(ref, ref, sem, sem, sib).wait_recv()

    def sent(ref, sem):
        send(ref, ref, sem, sem, sib).wait_send()

    loads = {}
    for i, (name, src, dst) in enumerate(
        (
            ("tok", tok_h, tok), ("tab", tab_h, tab), ("seg", seg_h, seg), ("cot", cot_h, cot),
            ("wdn", wdn_h, wdn), ("wup", wup_h, wup), ("bias", bias_h, bias),
        )
    ):
        loads[name] = pltpu.make_async_copy(src, dst, in_s.at[i])
        loads[name].start()

    bar = pltpu.get_barrier_semaphore()
    for d in range(1, 8):
        pl.semaphore_signal(bar, inc=1, device_id=at_w(d), device_id_type=MESH)
        pl.semaphore_signal(bar, inc=1, device_id=at_z(d), device_id_type=MESH)
    for d in range(1, 4):
        pl.semaphore_signal(bar, inc=1, device_id=at_x(d), device_id_type=MESH)

    loads["tok"].wait()

    @pl.loop(0, 9)
    def _(b):
        v = tok[rows_at(b * 128, 128, 128), :].astype(F32)
        s1 = v[:, 0:128]
        s2 = v[:, 0:128] * v[:, 0:128]
        for k in range(1, 5):
            p = v[:, k * 128 : (k + 1) * 128]
            s1 = s1 + p
            s2 = s2 + p * p
        lanes = rows_at(b * 128, 128, 128)
        stat[w, 0:1, lanes] = jnp.sum(s1.T, 0, keepdims=True)
        stat[w, 1:2, lanes] = jnp.sum(s2.T, 0, keepdims=True)

    row = lax.broadcasted_iota(jnp.int32, (R, NS), 0)
    picked = jnp.zeros((R, NS), jnp.int32)
    for r in range(R):
        picked = jnp.where(row == r, stp[r], picked)
    step_of = (picked == lax.broadcasted_iota(jnp.int32, (R, NS), 1)).astype(F32).astype(BF16)
    loads["tab"].wait()
    for k in range(3):
        parts = split3(tab[k])
        rm = dot(step_of, parts[0]) + dot(step_of, parts[1]) + dot(step_of, parts[2])
        for i, piece in enumerate(split3(rm)):
            rmod[k, i * R : (i + 1) * R, :] = piece

    pl.semaphore_wait(bar, 17)
    for d in range(1, 8):
        send(stat.at[w], stat.at[w], st_s.at[0], st_r.at[0], at_w(d)).start()

    loads["seg"].wait()
    loads["cot"].wait()

    @pl.loop(0, 9)
    def _(b):
        lanes = rows_at(b * 128, 128, 128)
        ids = jnp.broadcast_to(seg[lanes].reshape(1, 128), (R, 128))
        one = (ids == lax.broadcasted_iota(jnp.int32, (R, 128), 0)).astype(F32)
        oht[:, lanes] = one.astype(BF16)
        three = jnp.concatenate([one, one, one], 0)
        oh[lanes, :] = three.T.astype(BF16)
        gate = dot(oh[lanes, :], rmod[2])
        dout[lanes, :] = (cot[lanes, :].astype(F32) * gate).astype(BF16)

    def base(b, k):
        return 8 * OFF[b] + k * 4 * OB[b]

    def part(b):
        return slice(OFF[b], OFF[b] + OB[b])

    def four(b):
        return slice(4 * OFF[b], 4 * OFF[b] + 4 * OB[b])

    def target(b, d):
        return rows_at(4 * OFF[b] + ((y + d) % 4) * OB[b], OB[b])

    LO, HI = slice(0, YCUT), slice(YCUT, FW)
    cx = {}

    def to_core(a, b, left, right):
        psib[a, four(b)] = dot(left[rows_at(base(b, 1 - c), 4 * OB[b]), :], right[...], ((1,), (1,))).astype(BF16)
        cx[a, b] = send(psib.at[a, four(b)], rsib.at[a, four(b)], cx_s.at[a, b], cx_r.at[a, b], sib)
        cx[a, b].start()

    def to_opposite(a, b, left, right):
        p = dot(left[rows_at(base(b, c), 4 * OB[b]), :], right[...], ((1,), (1,)))
        cx[a, b].wait()
        pown[a, four(b)] = p + rsib[a, four(b)].astype(F32)
        yo[a, part(b)] = pown[a, target(b, 2), :].astype(BF16)
        for lanes, k, d in ((LO, 0, 1), (HI, 1, 3)):
            send(
                yo.at[a, part(b), lanes], yh.at[a, part(b), lanes], y_s.at[a, b], yh_r.at[a, b, k], at_y(d)
            ).start()

    def to_neighbours(a, b):
        for lanes, rest, k, d in ((LO, HI, 0, 1), (HI, LO, 1, 3)):
            received(yh.at[a, part(b), lanes], yh_r.at[a, b, k])
            mine = pown[a, target(b, d), :]
            ys[a, k, part(b), lanes] = (mine[:, lanes] + yh[a, part(b), lanes].astype(F32)).astype(BF16)
            ys[a, k, part(b), rest] = mine[:, rest].astype(BF16)
            send(
                ys.at[a, k, part(b)], yr.at[a, k, part(b)], y_s.at[a, b], yr_r.at[a, b, k], at_y(d)
            ).start()

    loads["wdn"].wait()
    for b in range(NB):
        to_core(0, b, dout, wdn)
    for b in range(NB):
        to_opposite(0, b, dout, wdn)

    received(stat.at[0:7], st_r.at[0])
    tot = stat[0]
    for k in range(1, 8):
        tot = tot + stat[k]
    mu = tot[0:1] / D
    inv = lax.rsqrt(tot[1:2] / D - mu * mu + 1e-06)
    mu8 = jnp.broadcast_to(mu, (8, T))
    inv8 = jnp.broadcast_to(inv, (8, T))
    for b in range(9):
        lanes = slice(b * 128, (b + 1) * 128)
        col[0, lanes, :] = mu8[:, lanes].T
        col[1, lanes, :] = inv8[:, lanes].T

    def normalize(first, last):
        @pl.loop(first, last)
        def _(b):
            rows = rows_at(b * 128, 128, 128)
            shift = dot(oh[rows, :], rmod[0])
            gain = 1.0 + dot(oh[rows, :], rmod[1])
            xh = (tok[rows, :].astype(F32) - col[0, rows, 0:1]) * col[1, rows, 0:1]
            nrm[rows, :] = (xh * gain + shift).astype(BF16)

    loads["wup"].wait()
    loads["bias"].wait()
    unit = 0
    for b in range(NB):
        normalize(unit, unit + UNITS[b])
        unit += UNITS[b]
        to_core(1, b, nrm, wup)
        to_neighbours(0, b)
    for b in range(NB):
        to_opposite(1, b, nrm, wup)

    def total(a, b):
        v = pown[a, target(b, 0), :]
        for k in range(2):
            v = v + yr[a, k, part(b)].astype(F32)
        return v

    def chunk(b, k, d):
        return rows_at(base(b, k) + ((y + d) % 4) * OB[b], OB[b])

    def activate(b):
        for a in range(2):
            for k in range(2):
                received(yr.at[a, k, part(b)], yr_r.at[a, b, k])
        pre = total(1, b) + bias[...]
        sq = pre * pre
        th = jnp.tanh(ROOT * (pre + CUBE * (sq * pre)))
        slope = 0.5 * (1.0 + th) + (0.5 * ROOT) * pre * (1.0 - th * th) * (1.0 + (3.0 * CUBE) * sq)
        had[1, chunk(b, c, 0), :] = (total(0, b) * slope).astype(BF16)
        had[0, chunk(b, c, 0), :] = (0.5 * pre * (1.0 + th)).astype(BF16)

    def pass_on(g, b, d, lanes, r_sem, dev):
        ref = had.at[g, chunk(b, c, d), lanes]
        send(ref, ref, ag_s.at[g, b], r_sem, dev).start()

    ALL = slice(0, FW)

    def spread_first(g, b):
        pass_on(g, b, 0, ALL, a1_r.at[g, b, 0], at_y(1))
        pass_on(g, b, 0, ALL, a1_r.at[g, b, 1], at_y(3))
        pass_on(g, b, 0, ALL, fw_r.at[g, b], sib)

    def spread_second(g, b):
        for k, d, to, lanes in ((0, 3, 1, LO), (1, 1, 3, HI)):
            received(had.at[g, chunk(b, c, d), :], a1_r.at[g, b, k])
            pass_on(g, b, d, lanes, a2_r.at[g, b, k], at_y(to))
            pass_on(g, b, d, ALL, fw_r.at[g, b], sib)

    def spread_third(g, b):
        for k, lanes in ((0, LO), (1, HI)):
            received(had.at[g, chunk(b, c, 2), lanes], a2_r.at[g, b, k])
        pass_on(g, b, 2, ALL, fw_r.at[g, b], sib)

    def spread_done(g, b):
        received(had.at[g, rows_at(base(b, 1 - c), 4 * OB[b]), :], fw_r.at[g, b])

    def zrow(b, d):
        return rows_at(8 * OFF[b] + ((z + d) % 8) * OB[b], OB[b])

    def norm_part(b):
        block = slice(8 * OFF[b], 8 * (OFF[b] + OB[b]))
        dn[block, :] = dot(had[1, block], wup[...])

    def zlanes(k, half):
        if not half:
            return slice(0, DW)
        return slice(0, CUT) if k == 0 else slice(CUT, DW)

    def hop(b, s):
        n = OB[b]
        for k, sign, to in ((0, -1, 1), (1, 1, 7)):
            mine = dn[zrow(b, 4 + sign * s), :]
            lanes = zlanes(k, s == 0)
            slot = k * 4 + s
            if s > 0:
                came = zlanes(k, s == 1)
                received(rb.at[b, slot - 1, 0:n, came], zr_r.at[b, slot - 1])
                if s == 1:
                    rest = zlanes(1 - k, True)
                    sb[b, slot, 0:n, rest] = mine[:, rest].astype(BF16)
                sb[b, slot, 0:n, came] = (mine[:, came] + rb[b, slot - 1, 0:n, came].astype(F32)).astype(BF16)
            else:
                sb[b, slot, 0:n, lanes] = mine[:, lanes].astype(BF16)
            send(
                sb.at[b, slot, 0:n, lanes], rb.at[b, slot, 0:n, lanes], zr_s.at[b], zr_r.at[b, slot], at_z(to)
            ).start()

    def land(b):
        n = OB[b]
        v = dn[zrow(b, 0), :]
        for k in range(2):
            received(rb.at[b, 4 * k + 3, 0:n], zr_r.at[b, 4 * k + 3])
            v = v + rb[b, 4 * k + 3, 0:n].astype(F32)
        xa[b, x, 0:n] = v.astype(BF16)
        ref = xa.at[b, x, 0:n]
        for d in (2, 1, 3):
            send(ref, ref, xe_s.at[b], xe_r.at[b], at_x(d)).start()

    def modul(b):
        rows = zrow(b, 0)
        gain = 1.0 + dot(oh[rows, :], rmod[1])
        rstd = col[1, rows, 0:1]
        xh = (tok[rows, :].astype(F32) - col[0, rows, 0:1]) * rstd
        return rows, gain, rstd, xh

    def finish_sums(b):
        n = OB[b]
        received(xa.at[b, 0:3, 0:n], xe_r.at[b])
        v = [xa[b, k, 0:n].astype(F32) for k in range(4)]
        v = (v[0] + v[1]) + (v[2] + v[3])
        rows, gain, rstd, xh = modul(b)
        dh = v * gain
        dhv[b, 0:n] = dh
        dhx = dh * xh
        s1 = dh[:, 0:128]
        s2 = dhx[:, 0:128]
        for k in range(1, 5):
            s1 = s1 + dh[:, k * 128 : (k + 1) * 128]
            s2 = s2 + dhx[:, k * 128 : (k + 1) * 128]
        both = jnp.concatenate([s1, s2, jnp.zeros((128 - 2 * n, 128), F32)], 0)
        mst[b, w] = jnp.sum(both.T, 0, keepdims=True)
        ref = mst.at[b, w]
        for d in range(1, 8):
            send(ref, ref, ms_s.at[b], ms_r.at[b], at_w(d)).start()

    def finish_rows(b):
        received(mst.at[b, 0:7], ms_r.at[b])
        n = OB[b]
        m = mst[b, 0]
        for k in range(1, 8):
            m = m + mst[b, k]
        mt = jnp.broadcast_to(m / D, (8, 128)).T
        rows, _, rstd, xh = modul(b)
        grad = cot[rows, :].astype(F32) + rstd * (dhv[b, 0:n] - mt[0:n, 0:1] - xh * mt[n : 2 * n, 0:1])
        gx[rows, :] = grad.astype(BF16)

    def ring(b, s):
        for k, sign, to in ((0, -1, 1), (1, 1, 7)):
            if s > 0:
                received(gx.at[zrow(b, 8 + sign * s), zlanes(k, s == 4)], zg_r.at[b, k, s - 1])
            if s < 4:
                ref = gx.at[zrow(b, 8 + sign * s), zlanes(k, s == 3)]
                send(ref, ref, zg_s.at[b], zg_r.at[b, k, s], at_z(to)).start()

    def table_block(b, carry):
        rows = rows_at(b * 128, 128, 128)
        dv = dn[rows, :]
        xh = (tok[rows, :].astype(F32) - col[0, rows, 0:1]) * col[1, rows, 0:1]
        yv = dot(had[0, rows, :], wdn[...]) * cot[rows, :].astype(F32)
        hot = oht[:, rows]
        out = []
        for acc, v in zip(carry, (dv, dv * xh, yv)):
            hi = v.astype(BF16)
            lo = (v - hi.astype(F32)).astype(BF16)
            out.append(acc + dot(hot, hi) + dot(hot, lo))
        return tuple(out)

    def kind_out(k):
        return send(
            tx.at[k, 3], tx.at[k, (x + 3 - k) % 4], tx_s.at[k], tx_r.at[0], (w, z * 4 + k)
        )

    def weight_gradient(out, left, right):
        for m in range(4):
            n = min(128, FW - m * 128)
            out[m * 128 : m * 128 + n, :] = dot(left[:, m * 128 : m * 128 + n], right[...], ((0,), (0,)))

    to_neighbours(1, 0)
    to_neighbours(1, 1)
    activate(0)
    spread_first(1, 0)
    to_neighbours(1, 2)
    activate(1)
    spread_first(1, 1)
    spread_second(1, 0)
    activate(2)
    spread_first(1, 2)
    spread_second(1, 1)
    spread_third(1, 0)
    spread_done(1, 0)
    norm_part(0)
    hop(0, 0)
    spread_second(1, 2)
    spread_third(1, 1)
    for b in range(NB):
        spread_first(0, b)
    spread_done(1, 1)
    norm_part(1)
    hop(1, 0)
    hop(0, 1)
    spread_third(1, 2)
    spread_done(1, 2)
    norm_part(2)
    hop(2, 0)
    spread_second(0, 0)
    hop(1, 1)
    hop(0, 2)
    spread_second(0, 1)
    hop(2, 1)
    spread_second(0, 2)
    hop(1, 2)
    spread_third(0, 0)
    hop(0, 3)
    spread_third(0, 1)
    hop(2, 2)
    spread_third(0, 2)
    zero = jnp.zeros((R, DW), F32)
    spread_done(0, 0)
    sums = lax.fori_loop(0, 2, table_block, (zero, zero, zero))
    hop(1, 3)
    land(0)
    spread_done(0, 1)
    spread_done(0, 2)
    sums = lax.fori_loop(2, 4, table_block, sums)
    hop(2, 3)
    land(1)
    finish_sums(0)
    sums = lax.fori_loop(4, 6, table_block, sums)
    land(2)
    finish_rows(0)
    ring(0, 0)
    finish_sums(1)
    sums = lax.fori_loop(6, 9, table_block, sums)

    for k in range(3):
        for q in range(8):
            tx[k, 3, q] = sums[k][2 * q : 2 * q + 2]
    for k in range(3):
        @pl.when(x != k)
        def _():
            kind_out(k).start()

    finish_sums(2)
    finish_rows(1)
    ring(1, 0)
    ring(0, 1)
    finish_rows(2)
    ring(2, 0)
    ring(1, 1)
    ring(0, 2)

    @pl.when(x < 3)
    def _():
        received(tx.at[0, 0:3], tx_r.at[0])
        tz[8] = (tx[x, 0] + tx[x, 1]) + (tx[x, 2] + tx[x, 3])
        for d in range(1, 8):
            send(tz.at[8, (z + d) % 8], tz.at[z, 0], tz_s.at[0], tz_r.at[0], at_z(d)).start()

    weight_gradient(gdn, had[0], dout)
    ring(2, 1)
    ring(1, 2)
    ring(0, 3)

    @pl.when(x < 3)
    def _():
        received(tz.at[0:7, 0], tz_r.at[0])
        sent(tz.at[0:7, 0], tz_s.at[0])
        tz[z, 0] = tz[8, z]
        v = tz[0, 0]
        for k in range(1, 8):
            v = v + tz[k, 0]
        tf[x, z] = v
        for d in range(1, 8):
            send(tf.at[x, z], tf.at[x, z], tg_s.at[0], tg_r.at[0], at_z(d)).start()

    weight_gradient(gup, had[1], nrm)
    ring(2, 2)
    ring(1, 3)

    @pl.when(x < 3)
    def _():
        received(tf.at[x, 0:7], tg_r.at[0])
        sent(tf.at[x, 0:7], tg_s.at[0])
        for d in range(1, 4):
            send(tf.at[x], tf.at[x], tb_s.at[0], tb_r.at[x], at_x(d)).start()

    gb[...] = dot(jnp.ones((8, T), BF16), had[1])[0:1]
    ring(2, 3)
    sent(stat.at[0:7], st_s.at[0])
    for b in range(NB):
        n = OB[b]
        for a in range(2):
            sent(psib.at[a, 0 : 3 * n], y_s.at[a, b])
            sent(had.at[a, 0 : 7 * n], ag_s.at[a, b])
        sent(sb.at[b, 0:7, 0:n], zr_s.at[b])
        sent(xa.at[b, 0:3, 0:n], xe_s.at[b])
        sent(mst.at[b, 0:7], ms_s.at[b])

    for k in range(3):
        @pl.when(x != k)
        def _():
            received(tf.at[k], tb_r.at[k])
            kind_out(k).wait_send()

    @pl.when(x < 3)
    def _():
        sent(tf.at[0:3], tb_s.at[0])

    for k in range(3):
        for q in range(8):
            comp[k, 2 * q : 2 * q + 2, :] = tf[k, q]
        out = jnp.zeros((NS, DW), F32)
        for p in split3(comp[k]):
            out = out + dot(step_of, p, ((0,), (0,)))
        gtab[k] = out

    for b in range(NB):
        ring(b, 4)
        sent(gx.at[0 : 7 * OB[b]], zg_s.at[b])


def flush(*refs):
    copies = [pltpu.make_async_copy(refs[k], refs[5 + k], refs[10].at[k]) for k in range(5)]
    for cp in copies:
        cp.start()
    for cp in copies:
        cp.wait()


def per_device(tokens, cotangent, w_up, bias_up, w_down, mod_table, seg_ids, step_ids):
    vm = pl.BlockSpec(memory_space=pltpu.VMEM)
    sm = pl.BlockSpec(memory_space=pltpu.SMEM)
    hbm = pl.BlockSpec(memory_space=pltpu.HBM)
    dma = pltpu.SemaphoreType.DMA
    shapes = (
        jax.ShapeDtypeStruct((T, DW), BF16),
        jax.ShapeDtypeStruct((FW, DW), F32),
        jax.ShapeDtypeStruct((FW, DW), F32),
        jax.ShapeDtypeStruct((1, FW), F32),
        jax.ShapeDtypeStruct((3, NS, DW), F32),
    )
    outs = pl.pallas_call(
        kernel,
        out_shape=shapes,
        in_specs=[hbm] * 7 + [sm],
        out_specs=(vm,) * 5,
        scratch_shapes=[
            pltpu.VMEM((T, DW), BF16),
            pltpu.VMEM((T, DW), BF16),
            pltpu.VMEM((FW, DW), BF16),
            pltpu.VMEM((1, FW), F32),
            pltpu.VMEM((FW, DW), BF16),
            pltpu.VMEM((3, NS, DW), F32),
            pltpu.VMEM((T,), jnp.int32),
            pltpu.VMEM((8, 2, T), F32),
            pltpu.VMEM((3, 3 * R, DW), BF16),
            pltpu.VMEM((T, 3 * R), BF16),
            pltpu.VMEM((R, T), BF16),
            pltpu.VMEM((2, T, 8), F32),
            pltpu.VMEM((T, DW), BF16),
            pltpu.VMEM((T, DW), BF16),
            pltpu.VMEM((2, 4 * CH, FW), BF16),
            pltpu.VMEM((2, 4 * CH, FW), BF16),
            pltpu.VMEM((2, 4 * CH, FW), F32),
            pltpu.VMEM((2, CH, FW), BF16),
            pltpu.VMEM((2, CH, FW), BF16),
            pltpu.VMEM((2, 2, CH, FW), BF16),
            pltpu.VMEM((2, 2, CH, FW), BF16),
            pltpu.VMEM((2, T, FW), BF16),
            pltpu.VMEM((T, DW), F32),
            pltpu.VMEM((NB, 8, OB[0], DW), BF16),
            pltpu.VMEM((NB, 8, OB[0], DW), BF16),
            pltpu.VMEM((NB, 4, OB[0], DW), BF16),
            pltpu.VMEM((NB, OB[0], DW), F32),
            pltpu.VMEM((NB, 8, 1, 128), F32),
            pltpu.VMEM((3, 4, 8, 2, DW), F32),
            pltpu.VMEM((9, 8, 2, DW), F32),
            pltpu.VMEM((3, 8, 2, DW), F32),
            pltpu.VMEM((3, R, DW), F32),
            dma((7,)),
            dma((1,)), dma((1,)),
            dma((2, NB)), dma((2, NB)),
            dma((2, NB)), dma((2, NB, 2)), dma((2, NB, 2)),
            dma((2, NB)), dma((2, NB, 2)), dma((2, NB, 2)), dma((2, NB)),
            dma((NB,)), dma((NB, 8)),
            dma((NB,)), dma((NB,)),
            dma((NB,)), dma((NB,)),
            dma((NB,)), dma((NB, 2, 4)),
            dma((3,)), dma((1,)),
            dma((1,)), dma((1,)),
            dma((1,)), dma((1,)),
            dma((1,)), dma((3,)),
        ],
        compiler_params=pltpu.CompilerParams(
            collective_id=0, has_side_effects=True, vmem_limit_bytes=34 * 1024 * 1024
        ),
        name="mlp_backward",
    )(
        *(
            pltpu.with_memory_space_constraint(v, pltpu.HBM)
            for v in (tokens, cotangent, w_up.T, bias_up[None, :], w_down, mod_table.transpose(1, 0, 2), seg_ids)
        ),
        step_ids,
    )
    outs = pl.pallas_call(
        flush,
        out_shape=shapes,
        in_specs=[vm] * 5,
        out_specs=(hbm,) * 5,
        scratch_shapes=[dma((5,))],
        compiler_params=pltpu.CompilerParams(vmem_limit_bytes=1024 * 1024),
        name="write_out",
    )(*outs)
    return outs[0], outs[1].T, outs[2], outs[3][0], outs[4].transpose(1, 0, 2)


def solution(mesh):
    placed = (
        P(None, "width"),
        P(None, "width"),
        P("width", "hidden"),
        P("hidden"),
        P("hidden", "width"),
        P(None, None, "width"),
        P(),
        P(),
    )
    return jax.shard_map(
        per_device,
        mesh=mesh,
        in_specs=placed,
        out_specs=(
            P(None, "width"),
            P("width", "hidden"),
            P("hidden", "width"),
            P("hidden"),
            P(None, None, "width"),
        ),
        check_vma=False,
    )
```

time: 339 us -> 89.5 us (0.26)
  waiting for transfers between devices: 234 us -> 0 us
  Pallas kernels: 0 us -> 88.1 us
  blocking collectives: 43.5 us -> 0 us
  matrix products: 29.6 us -> 0 us
  other arithmetic: 13.7 us -> 0 us
  between operations: 14.2 us -> 0.65 us
    psum x2 -> x0, waiting for transfers between devices: 234 us -> none  [the longest x1 156 us: per_device(): d_norm = lax.psum(d_part, 'hidden')]
    pallas_call x0 -> x2, Pallas kernels: none -> 88.1 us  [the longest x1 86.2 us: per_device(): pl.pallas_call(kernel, out_shape=shapes, in_specs=[hbm] * 7 + [sm], out_s...]
    psum x2 -> x0, blocking collectives: 43.5 us -> none  [the longest x1 22.8 us: per_device(): lax.psum((jnp.sum(x_full, 1), jnp.sum(x_full * x_full, 1)), 'width')]
    dot_general x14 -> x0, matrix products: 29.6 us -> none  [the longest x1 3.85 us: per_device(): down_part = jnp.dot(d_out, w_down.T, preferred_element_type=jnp.float32)]
    reduce_sum x3 -> x0, other arithmetic: 9.48 us -> none  [the longest x1 5.31 us: norm_back(): jnp.sum(d_hat, 1)]
    convert_element_type x1 -> x0, other arithmetic: 3.5 us -> none  [norm_back(): return grad_rows.astype(jnp.bfloat16)]
  transfers between devices with their start and end apart: 2 -> 0, of which waited for: 2 -> 0; matrix products, arithmetic and copies ran while one was open for 1% -> 0% of each run, Pallas kernels for 0% -> 0%
where the time goes in v3:
time: 89.5 us; the launch traced here: 89.4 us
  Pallas kernels  88.1 us (98%)
    pallas_call x1, Pallas kernels, per_device(): pl.pallas_call(kernel, out_shape=shapes, in_specs=[hbm] * 7 + [sm], out_s...  86.2 us
    pallas_call x1, Pallas kernels, per_device(): pl.pallas_call(flush, out_shape=shapes, in_specs=[vm] * 5, out_specs=(hbm...  1.96 us

profile of v3, /device:TPU:8, one launch (start us, length us, event | category | flops | bytes accessed | tf_op | source)
XLA Modules:
  0.0 89.4 jit_solution(11900627350592061847)
XLA Ops:
  0.6 0.0 copy-start
  0.6 0.6 copy-done
  1.3 86.2 %mlp_backward.1 = (bf16[1152,640]{1,0:T(8,128)(2,1)S(1)}, f32[432,640]{1,0:T(8,128)S(1)}, f32[432,640]{1,0:T(8,128)S(1)}, f32[1,432]{1,0:T(1,128)S(1)}, f32[3,32,640]{2,1,0:T(8,128)S(1)}) custom-call(bf16[1152,640]{1,0:T(8,128)(2,1)} %tok_h.1, bf16[1152,640]{1,0:T(8,128)(2,1)} %cot_h.1, bf16[432,640]{1,0:T(8,128)(2,1)} %bitcast.6, f32[1,432]{1,0:T(1,128)} %bitcast.8, ...), custom_call_target="tpu_custom_call" | custom-call | tf_op jit(solution)/shard_map/mlp_backward/pallas_call | solution.py:544
  87.5 2.0 %write_out.1 = (bf16[1152,640]{1,0:T(8,128)(2,1)}, f32[432,640]{1,0:T(8,128)}, f32[432,640]{1,0:T(8,128)}, f32[1,432]{1,0:T(1,128)}, f32[3,32,640]{2,1,0:T(8,128)}) custom-call(bf16[1152,640]{1,0:T(8,128)(2,1)S(1)} %get-tuple-element.15.refs_0_, f32[432,640]{1,0:T(8,128)S(1)} %get-tuple-element.16.refs_1_, f32[432,640]{1,0:T(8,128)S(1)} %get-tuple-element.17.refs_2_, ...), custom_call_target="tpu_custom_call" | custom-call | tf_op jit(solution)/shard_map/write_out/pallas_call | solution.py:607
Async XLA Ops:
  0.6 0.7 copy-start

commit v4 on v3

--- a/solution.py
+++ b/solution.py
@@ -18,7 +18,6 @@
 OFF = tuple(sum(OB[:b]) for b in range(NB))
 CH = sum(OB)
 CUT = 384
-YCUT = 256
 ROOT = 0.7978845608028654
 CUBE = 0.044715
 
@@ -39,14 +38,14 @@
 
 
 def kernel(
-    tok_h, cot_h, wup_h, bias_h, wdn_h, tab_h, seg_h, stp,
+    tok_h, cot_h, wup_h, bias_h, wdn_h, tab_h, seg_h, stp_h,
     gx, gup, gdn, gb, gtab,
-    tok, cot, wup, bias, wdn, tab, seg,
+    tok, cot, wup, bias, wdn, tab, seg, stp,
     stat, rmod, oh, oht, col, dout, nrm,
-    psib, rsib, pown, yo, yh, ys, yr, had,
+    psib, rsib, pown, ys, yr, had,
     dn, sb, rb, xa, dhv, mst,
     tx, tz, tf, comp,
-    in_s, st_s, st_r, cx_s, cx_r, y_s, yh_r, yr_r, ag_s, a1_r, a2_r, fw_r,
+    in_s, st_s, st_r, cx_s, cx_r, y_s, yr_r, ag_s, a1_r, fw_r,
     zr_s, zr_r, xe_s, xe_r, ms_s, ms_r, zg_s, zg_r,
     tx_s, tx_r, tz_s, tz_r, tg_s, tg_r, tb_s, tb_r,
 ):
@@ -83,7 +82,7 @@
     loads = {}
     for i, (name, src, dst) in enumerate(
         (
-            ("tok", tok_h, tok), ("tab", tab_h, tab), ("seg", seg_h, seg), ("cot", cot_h, cot),
+            ("tok", tok_h, tok), ("stp", stp_h, stp), ("tab", tab_h, tab), ("seg", seg_h, seg), ("cot", cot_h, cot),
             ("wdn", wdn_h, wdn), ("wup", wup_h, wup), ("bias", bias_h, bias),
         )
     ):
@@ -112,35 +111,34 @@
         stat[w, 0:1, lanes] = jnp.sum(s1.T, 0, keepdims=True)
         stat[w, 1:2, lanes] = jnp.sum(s2.T, 0, keepdims=True)
 
-    row = lax.broadcasted_iota(jnp.int32, (R, NS), 0)
-    picked = jnp.zeros((R, NS), jnp.int32)
-    for r in range(R):
-        picked = jnp.where(row == r, stp[r], picked)
-    step_of = (picked == lax.broadcasted_iota(jnp.int32, (R, NS), 1)).astype(F32).astype(BF16)
+    pl.semaphore_wait(bar, 17)
+    for d in range(1, 8):
+        send(stat.at[w], stat.at[w], st_s.at[0], st_r.at[0], at_w(d)).start()
+
+    loads["stp"].wait()
+    ids = jnp.broadcast_to(stp[...].reshape(1, R), (NS, R))
+    step_of = (ids == lax.broadcasted_iota(jnp.int32, (NS, R), 0)).astype(F32).astype(BF16)
     loads["tab"].wait()
     for k in range(3):
         parts = split3(tab[k])
-        rm = dot(step_of, parts[0]) + dot(step_of, parts[1]) + dot(step_of, parts[2])
+        rm = sum(dot(step_of, piece, ((0,), (0,))) for piece in parts)
         for i, piece in enumerate(split3(rm)):
             rmod[k, i * R : (i + 1) * R, :] = piece
 
-    pl.semaphore_wait(bar, 17)
-    for d in range(1, 8):
-        send(stat.at[w], stat.at[w], st_s.at[0], st_r.at[0], at_w(d)).start()
-
-    loads["seg"].wait()
-    loads["cot"].wait()
-
-    @pl.loop(0, 9)
-    def _(b):
-        lanes = rows_at(b * 128, 128, 128)
-        ids = jnp.broadcast_to(seg[lanes].reshape(1, 128), (R, 128))
-        one = (ids == lax.broadcasted_iota(jnp.int32, (R, 128), 0)).astype(F32)
-        oht[:, lanes] = one.astype(BF16)
-        three = jnp.concatenate([one, one, one], 0)
-        oh[lanes, :] = three.T.astype(BF16)
-        gate = dot(oh[lanes, :], rmod[2])
-        dout[lanes, :] = (cot[lanes, :].astype(F32) * gate).astype(BF16)
+    def units(b):
+        return sum(UNITS[:b]), sum(UNITS[: b + 1])
+
+    def outer(b):
+        @pl.loop(*units(b))
+        def _(i):
+            lanes = rows_at(i * 128, 128, 128)
+            ids = jnp.broadcast_to(seg[lanes].reshape(1, 128), (R, 128))
+            one = (ids == lax.broadcasted_iota(jnp.int32, (R, 128), 0)).astype(F32)
+            oht[:, lanes] = one.astype(BF16)
+            three = jnp.concatenate([one, one, one], 0)
+            oh[lanes, :] = three.T.astype(BF16)
+            gate = dot(oh[lanes, :], rmod[2])
+            dout[lanes, :] = (cot[lanes, :].astype(F32) * gate).astype(BF16)
 
     def base(b, k):
         return 8 * OFF[b] + k * 4 * OB[b]
@@ -154,7 +152,6 @@
     def target(b, d):
         return rows_at(4 * OFF[b] + ((y + d) % 4) * OB[b], OB[b])
 
-    LO, HI = slice(0, YCUT), slice(YCUT, FW)
     cx = {}
 
     def to_core(a, b, left, right):
@@ -162,68 +159,42 @@
         cx[a, b] = send(psib.at[a, four(b)], rsib.at[a, four(b)], cx_s.at[a, b], cx_r.at[a, b], sib)
         cx[a, b].start()
 
-    def to_opposite(a, b, left, right):
+    def to_chips(a, b, left, right):
         p = dot(left[rows_at(base(b, c), 4 * OB[b]), :], right[...], ((1,), (1,)))
         cx[a, b].wait()
         pown[a, four(b)] = p + rsib[a, four(b)].astype(F32)
-        yo[a, part(b)] = pown[a, target(b, 2), :].astype(BF16)
-        for lanes, k, d in ((LO, 0, 1), (HI, 1, 3)):
+        for d in (2, 1, 3):
+            ys[a, d - 1, part(b)] = pown[a, target(b, d), :].astype(BF16)
             send(
-                yo.at[a, part(b), lanes], yh.at[a, part(b), lanes], y_s.at[a, b], yh_r.at[a, b, k], at_y(d)
+                ys.at[a, d - 1, part(b)], yr.at[a, d - 1, part(b)], y_s.at[a, b], yr_r.at[a, b, d - 1], at_y(d)
             ).start()
 
-    def to_neighbours(a, b):
-        for lanes, rest, k, d in ((LO, HI, 0, 1), (HI, LO, 1, 3)):
-            received(yh.at[a, part(b), lanes], yh_r.at[a, b, k])
-            mine = pown[a, target(b, d), :]
-            ys[a, k, part(b), lanes] = (mine[:, lanes] + yh[a, part(b), lanes].astype(F32)).astype(BF16)
-            ys[a, k, part(b), rest] = mine[:, rest].astype(BF16)
-            send(
-                ys.at[a, k, part(b)], yr.at[a, k, part(b)], y_s.at[a, b], yr_r.at[a, b, k], at_y(d)
-            ).start()
-
-    loads["wdn"].wait()
-    for b in range(NB):
-        to_core(0, b, dout, wdn)
-    for b in range(NB):
-        to_opposite(0, b, dout, wdn)
-
-    received(stat.at[0:7], st_r.at[0])
-    tot = stat[0]
-    for k in range(1, 8):
-        tot = tot + stat[k]
-    mu = tot[0:1] / D
-    inv = lax.rsqrt(tot[1:2] / D - mu * mu + 1e-06)
-    mu8 = jnp.broadcast_to(mu, (8, T))
-    inv8 = jnp.broadcast_to(inv, (8, T))
-    for b in range(9):
-        lanes = slice(b * 128, (b + 1) * 128)
-        col[0, lanes, :] = mu8[:, lanes].T
-        col[1, lanes, :] = inv8[:, lanes].T
-
-    def normalize(first, last):
-        @pl.loop(first, last)
-        def _(b):
-            rows = rows_at(b * 128, 128, 128)
+    def columns():
+        received(stat.at[0:7], st_r.at[0])
+        tot = stat[0]
+        for k in range(1, 8):
+            tot = tot + stat[k]
+        mu = tot[0:1] / D
+        inv = lax.rsqrt(tot[1:2] / D - mu * mu + 1e-06)
+        mu8 = jnp.broadcast_to(mu, (8, T))
+        inv8 = jnp.broadcast_to(inv, (8, T))
+        for b in range(9):
+            lanes = slice(b * 128, (b + 1) * 128)
+            col[0, lanes, :] = mu8[:, lanes].T
+            col[1, lanes, :] = inv8[:, lanes].T
+
+    def normalize(b):
+        @pl.loop(*units(b))
+        def _(i):
+            rows = rows_at(i * 128, 128, 128)
             shift = dot(oh[rows, :], rmod[0])
             gain = 1.0 + dot(oh[rows, :], rmod[1])
             xh = (tok[rows, :].astype(F32) - col[0, rows, 0:1]) * col[1, rows, 0:1]
             nrm[rows, :] = (xh * gain + shift).astype(BF16)
 
-    loads["wup"].wait()
-    loads["bias"].wait()
-    unit = 0
-    for b in range(NB):
-        normalize(unit, unit + UNITS[b])
-        unit += UNITS[b]
-        to_core(1, b, nrm, wup)
-        to_neighbours(0, b)
-    for b in range(NB):
-        to_opposite(1, b, nrm, wup)
-
     def total(a, b):
         v = pown[a, target(b, 0), :]
-        for k in range(2):
+        for k in range(3):
             v = v + yr[a, k, part(b)].astype(F32)
         return v
 
@@ -232,7 +203,7 @@
 
     def activate(b):
         for a in range(2):
-            for k in range(2):
+            for k in range(3):
                 received(yr.at[a, k, part(b)], yr_r.at[a, b, k])
         pre = total(1, b) + bias[...]
         sq = pre * pre
@@ -241,27 +212,25 @@
         had[1, chunk(b, c, 0), :] = (total(0, b) * slope).astype(BF16)
         had[0, chunk(b, c, 0), :] = (0.5 * pre * (1.0 + th)).astype(BF16)
 
-    def pass_on(g, b, d, lanes, r_sem, dev):
-        ref = had.at[g, chunk(b, c, d), lanes]
+    def pass_on(g, b, d, r_sem, dev):
+        ref = had.at[g, chunk(b, c, d), :]
         send(ref, ref, ag_s.at[g, b], r_sem, dev).start()
 
-    ALL = slice(0, FW)
-
     def spread_first(g, b):
-        pass_on(g, b, 0, ALL, a1_r.at[g, b, 0], at_y(1))
-        pass_on(g, b, 0, ALL, a1_r.at[g, b, 1], at_y(3))
-        pass_on(g, b, 0, ALL, fw_r.at[g, b], sib)
+        for d in (2, 1, 3):
+            pass_on(g, b, 0, a1_r.at[g, b, d - 1], at_y(d))
+        pass_on(g, b, 0, fw_r.at[g, b], sib)
+
+    def spread_from(g, b, d):
+        received(had.at[g, chunk(b, c, 4 - d), :], a1_r.at[g, b, d - 1])
+        pass_on(g, b, 4 - d, fw_r.at[g, b], sib)
 
     def spread_second(g, b):
-        for k, d, to, lanes in ((0, 3, 1, LO), (1, 1, 3, HI)):
-            received(had.at[g, chunk(b, c, d), :], a1_r.at[g, b, k])
-            pass_on(g, b, d, lanes, a2_r.at[g, b, k], at_y(to))
-            pass_on(g, b, d, ALL, fw_r.at[g, b], sib)
+        spread_from(g, b, 1)
+        spread_from(g, b, 3)
 
     def spread_third(g, b):
-        for k, lanes in ((0, LO), (1, HI)):
-            received(had.at[g, chunk(b, c, 2), lanes], a2_r.at[g, b, k])
-        pass_on(g, b, 2, ALL, fw_r.at[g, b], sib)
+        spread_from(g, b, 2)
 
     def spread_done(g, b):
         received(had.at[g, rows_at(base(b, 1 - c), 4 * OB[b]), :], fw_r.at[g, b])
@@ -329,7 +298,8 @@
         for k in range(1, 5):
             s1 = s1 + dh[:, k * 128 : (k + 1) * 128]
             s2 = s2 + dhx[:, k * 128 : (k + 1) * 128]
-        both = jnp.concatenate([s1, s2, jnp.zeros((128 - 2 * n, 128), F32)], 0)
+        both = [s1, s2] + [jnp.zeros((128 - 2 * n, 128), F32)] * (n < 64)
+        both = jnp.concatenate(both, 0)
         mst[b, w] = jnp.sum(both.T, 0, keepdims=True)
         ref = mst.at[b, w]
         for d in range(1, 8):
@@ -377,62 +347,83 @@
             n = min(128, FW - m * 128)
             out[m * 128 : m * 128 + n, :] = dot(left[:, m * 128 : m * 128 + n], right[...], ((0,), (0,)))
 
-    to_neighbours(1, 0)
-    to_neighbours(1, 1)
+    loads["seg"].wait()
+    loads["cot"].wait()
+    outer(0)
+    loads["wdn"].wait()
+    to_core(0, 0, dout, wdn)
+    outer(1)
+    to_core(0, 1, dout, wdn)
+    to_chips(0, 0, dout, wdn)
+    columns()
+    normalize(0)
+    loads["wup"].wait()
+    to_core(1, 0, nrm, wup)
+    to_chips(1, 0, nrm, wup)
+    outer(2)
+    to_core(0, 2, dout, wdn)
+    to_chips(0, 1, dout, wdn)
+    normalize(1)
+    to_core(1, 1, nrm, wup)
+    to_chips(1, 1, nrm, wup)
+    loads["bias"].wait()
     activate(0)
     spread_first(1, 0)
-    to_neighbours(1, 2)
+    to_chips(0, 2, dout, wdn)
+    normalize(2)
+    to_core(1, 2, nrm, wup)
+    to_chips(1, 2, nrm, wup)
     activate(1)
     spread_first(1, 1)
     spread_second(1, 0)
-    activate(2)
-    spread_first(1, 2)
-    spread_second(1, 1)
     spread_third(1, 0)
     spread_done(1, 0)
     norm_part(0)
     hop(0, 0)
-    spread_second(1, 2)
+    activate(2)
+    spread_first(1, 2)
+    spread_second(1, 1)
     spread_third(1, 1)
-    for b in range(NB):
-        spread_first(0, b)
+    hop(0, 1)
     spread_done(1, 1)
     norm_part(1)
     hop(1, 0)
-    hop(0, 1)
+    spread_second(1, 2)
     spread_third(1, 2)
+    spread_first(0, 0)
+    spread_first(0, 1)
+    spread_first(0, 2)
+    hop(0, 2)
     spread_done(1, 2)
     norm_part(2)
     hop(2, 0)
+    hop(1, 1)
+    hop(0, 3)
+    hop(2, 1)
+    hop(1, 2)
+    land(0)
     spread_second(0, 0)
-    hop(1, 1)
-    hop(0, 2)
     spread_second(0, 1)
-    hop(2, 1)
     spread_second(0, 2)
-    hop(1, 2)
+    hop(2, 2)
+    hop(1, 3)
+    finish_sums(0)
     spread_third(0, 0)
-    hop(0, 3)
     spread_third(0, 1)
-    hop(2, 2)
     spread_third(0, 2)
-    zero = jnp.zeros((R, DW), F32)
+    land(1)
+    hop(2, 3)
+    finish_rows(0)
+    ring(0, 0)
     spread_done(0, 0)
-    sums = lax.fori_loop(0, 2, table_block, (zero, zero, zero))
-    hop(1, 3)
-    land(0)
     spread_done(0, 1)
     spread_done(0, 2)
-    sums = lax.fori_loop(2, 4, table_block, sums)
-    hop(2, 3)
-    land(1)
-    finish_sums(0)
-    sums = lax.fori_loop(4, 6, table_block, sums)
+    zero = jnp.zeros((R, DW), F32)
+    sums = lax.fori_loop(0, 4, table_block, (zero, zero, zero))
+    finish_sums(1)
     land(2)
-    finish_rows(0)
-    ring(0, 0)
-    finish_sums(1)
-    sums = lax.fori_loop(6, 9, table_block, sums)
+    ring(0, 1)
+    sums = lax.fori_loop(4, 9, table_block, sums)
 
     for k in range(3):
         for q in range(8):
@@ -442,14 +433,11 @@
         def _():
             kind_out(k).start()
 
-    finish_sums(2)
     finish_rows(1)
     ring(1, 0)
-    ring(0, 1)
-    finish_rows(2)
-    ring(2, 0)
+    finish_sums(2)
+    ring(0, 2)
     ring(1, 1)
-    ring(0, 2)
 
     @pl.when(x < 3)
     def _():
@@ -458,10 +446,10 @@
         for d in range(1, 8):
             send(tz.at[8, (z + d) % 8], tz.at[z, 0], tz_s.at[0], tz_r.at[0], at_z(d)).start()
 
-    weight_gradient(gdn, had[0], dout)
-    ring(2, 1)
+    finish_rows(2)
+    ring(2, 0)
+    ring(0, 3)
     ring(1, 2)
-    ring(0, 3)
 
     @pl.when(x < 3)
     def _():
@@ -475,8 +463,7 @@
         for d in range(1, 8):
             send(tf.at[x, z], tf.at[x, z], tg_s.at[0], tg_r.at[0], at_z(d)).start()
 
-    weight_gradient(gup, had[1], nrm)
-    ring(2, 2)
+    ring(2, 1)
     ring(1, 3)
 
     @pl.when(x < 3)
@@ -486,8 +473,11 @@
         for d in range(1, 4):
             send(tf.at[x], tf.at[x], tb_s.at[0], tb_r.at[x], at_x(d)).start()
 
+    ring(2, 2)
+    weight_gradient(gdn, had[0], dout)
+    weight_gradient(gup, had[1], nrm)
+    ring(2, 3)
     gb[...] = dot(jnp.ones((8, T), BF16), had[1])[0:1]
-    ring(2, 3)
     sent(stat.at[0:7], st_s.at[0])
     for b in range(NB):
         n = OB[b]
@@ -513,7 +503,7 @@
             comp[k, 2 * q : 2 * q + 2, :] = tf[k, q]
         out = jnp.zeros((NS, DW), F32)
         for p in split3(comp[k]):
-            out = out + dot(step_of, p, ((0,), (0,)))
+            out = out + dot(step_of, p)
         gtab[k] = out
 
     for b in range(NB):
@@ -531,7 +521,6 @@
 
 def per_device(tokens, cotangent, w_up, bias_up, w_down, mod_table, seg_ids, step_ids):
     vm = pl.BlockSpec(memory_space=pltpu.VMEM)
-    sm = pl.BlockSpec(memory_space=pltpu.SMEM)
     hbm = pl.BlockSpec(memory_space=pltpu.HBM)
     dma = pltpu.SemaphoreType.DMA
     shapes = (
@@ -544,7 +533,7 @@
     outs = pl.pallas_call(
         kernel,
         out_shape=shapes,
-        in_specs=[hbm] * 7 + [sm],
+        in_specs=[hbm] * 8,
         out_specs=(vm,) * 5,
         scratch_shapes=[
             pltpu.VMEM((T, DW), BF16),
@@ -554,6 +543,7 @@
             pltpu.VMEM((FW, DW), BF16),
             pltpu.VMEM((3, NS, DW), F32),
             pltpu.VMEM((T,), jnp.int32),
+            pltpu.VMEM((R,), jnp.int32),
             pltpu.VMEM((8, 2, T), F32),
             pltpu.VMEM((3, 3 * R, DW), BF16),
             pltpu.VMEM((T, 3 * R), BF16),
@@ -564,26 +554,24 @@
             pltpu.VMEM((2, 4 * CH, FW), BF16),
             pltpu.VMEM((2, 4 * CH, FW), BF16),
             pltpu.VMEM((2, 4 * CH, FW), F32),
-            pltpu.VMEM((2, CH, FW), BF16),
-            pltpu.VMEM((2, CH, FW), BF16),
-            pltpu.VMEM((2, 2, CH, FW), BF16),
-            pltpu.VMEM((2, 2, CH, FW), BF16),
+            pltpu.VMEM((2, 3, CH, FW), BF16),
+            pltpu.VMEM((2, 3, CH, FW), BF16),
             pltpu.VMEM((2, T, FW), BF16),
             pltpu.VMEM((T, DW), F32),
-            pltpu.VMEM((NB, 8, OB[0], DW), BF16),
-            pltpu.VMEM((NB, 8, OB[0], DW), BF16),
-            pltpu.VMEM((NB, 4, OB[0], DW), BF16),
-            pltpu.VMEM((NB, OB[0], DW), F32),
+            pltpu.VMEM((NB, 8, max(OB), DW), BF16),
+            pltpu.VMEM((NB, 8, max(OB), DW), BF16),
+            pltpu.VMEM((NB, 4, max(OB), DW), BF16),
+            pltpu.VMEM((NB, max(OB), DW), F32),
             pltpu.VMEM((NB, 8, 1, 128), F32),
             pltpu.VMEM((3, 4, 8, 2, DW), F32),
             pltpu.VMEM((9, 8, 2, DW), F32),
             pltpu.VMEM((3, 8, 2, DW), F32),
             pltpu.VMEM((3, R, DW), F32),
-            dma((7,)),
+            dma((8,)),
             dma((1,)), dma((1,)),
             dma((2, NB)), dma((2, NB)),
-            dma((2, NB)), dma((2, NB, 2)), dma((2, NB, 2)),
-            dma((2, NB)), dma((2, NB, 2)), dma((2, NB, 2)), dma((2, NB)),
+            dma((2, NB)), dma((2, NB, 3)),
+            dma((2, NB)), dma((2, NB, 3)), dma((2, NB)),
             dma((NB,)), dma((NB, 8)),
             dma((NB,)), dma((NB,)),
             dma((NB,)), dma((NB,)),
@@ -600,9 +588,8 @@
     )(
         *(
             pltpu.with_memory_space_constraint(v, pltpu.HBM)
-            for v in (tokens, cotangent, w_up.T, bias_up[None, :], w_down, mod_table.transpose(1, 0, 2), seg_ids)
+            for v in (tokens, cotangent, w_up.T, bias_up[None, :], w_down, mod_table.transpose(1, 0, 2), seg_ids, step_ids)
         ),
-        step_ids,
     )
     outs = pl.pallas_call(
         flush,

time: 89.5 us -> 84.7 us (0.946)
  Pallas kernels: 88.1 us -> 84 us
    pallas_call x1, Pallas kernels: 86.2 us -> 82 us  [per_device(): pl.pallas_call(kernel, out_shape=shapes, in_specs=[hbm] * 8, out_specs=(v...]
where the time goes in v4:
time: 84.7 us; the launch traced here: 84.6 us
  Pallas kernels  84 us (99%)
    pallas_call x1, Pallas kernels, per_device(): pl.pallas_call(kernel, out_shape=shapes, in_specs=[hbm] * 8, out_specs=(v...  82 us
    pallas_call x1, Pallas kernels, per_device(): pl.pallas_call(flush, out_shape=shapes, in_specs=[vm] * 5, out_specs=(hbm...  1.96 us

profile of v4, /device:TPU:8, one launch (start us, length us, event | category | flops | bytes accessed | tf_op | source)
XLA Modules:
  0.0 84.6 jit_solution(9430798343965225034)
XLA Ops:
  0.6 82.0 %mlp_backward.1 = (bf16[1152,640]{1,0:T(8,128)(2,1)S(1)}, f32[432,640]{1,0:T(8,128)S(1)}, f32[432,640]{1,0:T(8,128)S(1)}, f32[1,432]{1,0:T(1,128)S(1)}, f32[3,32,640]{2,1,0:T(8,128)S(1)}) custom-call(bf16[1152,640]{1,0:T(8,128)(2,1)} %tok_h.1, bf16[1152,640]{1,0:T(8,128)(2,1)} %cot_h.1, bf16[432,640]{1,0:T(8,128)(2,1)} %bitcast.6, f32[1,432]{1,0:T(1,128)} %bitcast.8, ...), custom_call_target="tpu_custom_call" | custom-call | tf_op jit(solution)/shard_map/mlp_backward/pallas_call | solution.py:533
  82.7 2.0 %write_out.1 = (bf16[1152,640]{1,0:T(8,128)(2,1)}, f32[432,640]{1,0:T(8,128)}, f32[432,640]{1,0:T(8,128)}, f32[1,432]{1,0:T(1,128)}, f32[3,32,640]{2,1,0:T(8,128)}) custom-call(bf16[1152,640]{1,0:T(8,128)(2,1)S(1)} %get-tuple-element.15.refs_0_, f32[432,640]{1,0:T(8,128)S(1)} %get-tuple-element.16.refs_1_, f32[432,640]{1,0:T(8,128)S(1)} %get-tuple-element.17.refs_2_, ...), custom_call_target="tpu_custom_call" | custom-call | tf_op jit(solution)/shard_map/write_out/pallas_call | solution.py:594

commit v5 on v4

--- a/solution.py
+++ b/solution.py
@@ -286,10 +286,10 @@
 
     def finish_sums(b):
         n = OB[b]
+        rows, gain, rstd, xh = modul(b)
         received(xa.at[b, 0:3, 0:n], xe_r.at[b])
         v = [xa[b, k, 0:n].astype(F32) for k in range(4)]
         v = (v[0] + v[1]) + (v[2] + v[3])
-        rows, gain, rstd, xh = modul(b)
         dh = v * gain
         dhv[b, 0:n] = dh
         dhx = dh * xh
@@ -306,13 +306,13 @@
             send(ref, ref, ms_s.at[b], ms_r.at[b], at_w(d)).start()
 
     def finish_rows(b):
+        n = OB[b]
+        rows, _, rstd, xh = modul(b)
         received(mst.at[b, 0:7], ms_r.at[b])
-        n = OB[b]
         m = mst[b, 0]
         for k in range(1, 8):
             m = m + mst[b, k]
         mt = jnp.broadcast_to(m / D, (8, 128)).T
-        rows, _, rstd, xh = modul(b)
         grad = cot[rows, :].astype(F32) + rstd * (dhv[b, 0:n] - mt[0:n, 0:1] - xh * mt[n : 2 * n, 0:1])
         gx[rows, :] = grad.astype(BF16)
 

time: 84.7 us -> 84.6 us (level)
  no operation moved by 1% of the time
where the time goes in v5:
time: 84.6 us; the launch traced here: 84.5 us
  Pallas kernels  83.9 us (99%)
    pallas_call x1, Pallas kernels, per_device(): pl.pallas_call(kernel, out_shape=shapes, in_specs=[hbm] * 8, out_specs=(v...  81.9 us
    pallas_call x1, Pallas kernels, per_device(): pl.pallas_call(flush, out_shape=shapes, in_specs=[vm] * 5, out_specs=(hbm...  1.96 us

profile of v5, /device:TPU:8, one launch (start us, length us, event | category | flops | bytes accessed | tf_op | source)
XLA Modules:
  0.0 84.5 jit_solution(9990909277861489606)
XLA Ops:
  0.6 81.9 %mlp_backward.1 = (bf16[1152,640]{1,0:T(8,128)(2,1)S(1)}, f32[432,640]{1,0:T(8,128)S(1)}, f32[432,640]{1,0:T(8,128)S(1)}, f32[1,432]{1,0:T(1,128)S(1)}, f32[3,32,640]{2,1,0:T(8,128)S(1)}) custom-call(bf16[1152,640]{1,0:T(8,128)(2,1)} %tok_h.1, bf16[1152,640]{1,0:T(8,128)(2,1)} %cot_h.1, bf16[432,640]{1,0:T(8,128)(2,1)} %bitcast.6, f32[1,432]{1,0:T(1,128)} %bitcast.8, ...), custom_call_target="tpu_custom_call" | custom-call | tf_op jit(solution)/shard_map/mlp_backward/pallas_call | solution.py:533
  82.6 2.0 %write_out.1 = (bf16[1152,640]{1,0:T(8,128)(2,1)}, f32[432,640]{1,0:T(8,128)}, f32[432,640]{1,0:T(8,128)}, f32[1,432]{1,0:T(1,128)}, f32[3,32,640]{2,1,0:T(8,128)}) custom-call(bf16[1152,640]{1,0:T(8,128)(2,1)S(1)} %get-tuple-element.15.refs_0_, f32[432,640]{1,0:T(8,128)S(1)} %get-tuple-element.16.refs_1_, f32[432,640]{1,0:T(8,128)S(1)} %get-tuple-element.17.refs_2_, ...), custom_call_target="tpu_custom_call" | custom-call | tf_op jit(solution)/shard_map/write_out/pallas_call | solution.py:594
